TPU v7x, 32 devices: a whole 2x2x4 slice. The times are simulated.
32 devices in a mesh: fsdp: 4 (over z), context: 4 (over y, x), tensor: 2 (over core).
Axes of the slice: x: 2, y: 2, z: 4, core: 2. Of those that a mesh axis runs over, the one named last changes fastest.
Arguments:
- tokens: int32 [3, 4, 1024], P(None, 'fsdp'), may hold values from 0 to 49151
- lengths: int32 [3, 4], P(None, 'fsdp'), may hold values from 1024 to 1024, as said below
- loss_positions: int32 [3, 4, 128], P(None, 'fsdp'), may hold values from 0 to 1023
- teacher_ids: int32 [3, 4, 128, 64], P(None, 'fsdp'), may hold values from 0 to 49151
- label_ids: int32 [3, 4, 128], P(None, 'fsdp'), may hold values from 0 to 49151
- embedding: float32 [49152, 960], P(('context', 'tensor')), may hold values from -0.375 to 0.375
- incoming: float32 [1, 960, 1600], P(None, ('fsdp', 'tensor')), may hold values from -0.1875 to 0.1875
- outgoing: float32 [1, 960, 960], P(None, ('fsdp', 'tensor')), may hold values from -1.5 to 1.5
- expand: float32 [1, 960, 5120], P(None, ('fsdp', 'tensor')), may hold values from -0.1875 to 0.1875
- contract: float32 [1, 2560, 960], P(None, ('fsdp', 'tensor')), may hold values from -0.125 to 0.125
- scales: float32 [3, 960], P(None, ('fsdp', 'tensor')), may hold values from 0.5 to 1.5
- drift_embedding: float32 [49152, 960], P(('context', 'tensor')), may hold values from -9.536743e-07 to 9.536743e-07
- incoming_first_moment: float32 [1, 960, 1600], P(None, ('fsdp', 'tensor')), may hold values from -9.536743e-07 to 9.536743e-07
- drift_outgoing: float32 [1, 960, 960], P(None, ('fsdp', 'tensor')), may hold values from -9.536743e-07 to 9.536743e-07
- drift_expand: float32 [1, 960, 5120], P(None, ('fsdp', 'tensor')), may hold values from -9.536743e-07 to 9.536743e-07
- drift_contract: float32 [1, 2560, 960], P(None, ('fsdp', 'tensor')), may hold values from -9.536743e-07 to 9.536743e-07
- drift_scales: float32 [3, 960], P(None, ('fsdp', 'tensor')), may hold values from -9.536743e-07 to 9.536743e-07
- power_embedding: float32 [49152, 960], P(('context', 'tensor')), may hold values from 9.2249626e-14 to 3.68297e-13
- incoming_second_moment: float32 [1, 960, 1600], P(None, ('fsdp', 'tensor')), may hold values from 9.2249626e-14 to 3.68297e-13
- power_outgoing: float32 [1, 960, 960], P(None, ('fsdp', 'tensor')), may hold values from 9.2249626e-14 to 3.68297e-13
- power_expand: float32 [1, 960, 5120], P(None, ('fsdp', 'tensor')), may hold values from 9.2249626e-14 to 3.68297e-13
- power_contract: float32 [1, 2560, 960], P(None, ('fsdp', 'tensor')), may hold values from 9.2249626e-14 to 3.68297e-13
- power_scales: float32 [3, 960], P(None, ('fsdp', 'tensor')), may hold values from 9.2249626e-14 to 3.68297e-13
Outputs:
- loss_value: float32 [], replicated
- grad_norm: float32 [], replicated
- next_embedding: float32 [49152, 960], P(('context', 'tensor'))
- next_incoming: float32 [1, 960, 1600], P(None, ('fsdp', 'tensor'))
- next_outgoing: float32 [1, 960, 960], P(None, ('fsdp', 'tensor'))
- next_expand: float32 [1, 960, 5120], P(None, ('fsdp', 'tensor'))
- next_contract: float32 [1, 2560, 960], P(None, ('fsdp', 'tensor'))
- next_scales: float32 [3, 960], P(None, ('fsdp', 'tensor'))
- moment_embedding: float32 [49152, 960], P(('context', 'tensor'))
- moment_incoming: float32 [1, 960, 1600], P(None, ('fsdp', 'tensor'))
- moment_outgoing: float32 [1, 960, 960], P(None, ('fsdp', 'tensor'))
- moment_expand: float32 [1, 960, 5120], P(None, ('fsdp', 'tensor'))
- moment_contract: float32 [1, 2560, 960], P(None, ('fsdp', 'tensor'))
- moment_scales: float32 [3, 960], P(None, ('fsdp', 'tensor'))
- square_embedding: float32 [49152, 960], P(('context', 'tensor'))
- square_incoming: float32 [1, 960, 1600], P(None, ('fsdp', 'tensor'))
- square_outgoing: float32 [1, 960, 960], P(None, ('fsdp', 'tensor'))
- square_expand: float32 [1, 960, 5120], P(None, ('fsdp', 'tensor'))
- square_contract: float32 [1, 2560, 960], P(None, ('fsdp', 'tensor'))
- square_scales: float32 [3, 960], P(None, ('fsdp', 'tensor'))
Inputs may be any that keep to these rules, and one draw needn't show every extreme that they name: `lengths`: in each of the 3 micro-batches one sequence has exactly 1024 tokens. `loss_positions`: a loss position is this value modulo the sequence's length.
All inputs are finite; a program needn't handle non-finite values.
Results may differ from a plain program's by a relative error of at most 0.0065.
The roundings to bfloat16 on the way count: a program that leaves them out, or rounds other values in their place, can miss the bound.
Values may be sent and summed in bfloat16 or wider, within the bound.
A program may use at most 512 MiB of HBM per device.

v0:
```python
import jax
import jax.numpy as jnp
from jax import lax
from jax.sharding import PartitionSpec as P

QUERY_HEADS = 15
KEY_VALUE_HEADS = 5
HEAD_SIZE = 64
FF = 2560
LAYER_COUNT = 1
TEACH = 64
STEP = 10


EPSILON = 1e-05
THETA = 100000.0
CLIP = 0.01
BETA_ONE = 0.9
BETA_TWO = 0.95
ADAM_EPSILON = 1e-08
DECAY = 0.1
RATE_MATRIX = 0.05
RATE_GAIN = 0.5
MASKED = -1e30


def shortened(value):

    def short(part):
        return part.astype(jnp.bfloat16) if part.dtype == jnp.float32 else part

    return jax.tree.map(short, value)


def merged(part, axis, combine):
    gathered = jax.tree.map(lambda a: lax.all_gather(a, axis), part)

    def take(source):
        return jax.tree.map(lambda a: lax.dynamic_index_in_dim(a, source, 0, False), gathered)

    return lax.fori_loop(
        1, lax.axis_size(axis), lambda source, state: combine(state, take(source)), take(0)
    )


def matmul(left, right):
    return jnp.dot(left, right, preferred_element_type=jnp.float32)


def across(left, right):
    return lax.dot_general(
        left, right, (((0,), (0,)), ((), ())), preferred_element_type=jnp.float32
    )


def against(left, right):
    return lax.dot_general(
        left, right, (((1,), (1,)), ((), ())), preferred_element_type=jnp.float32
    )


def rounded(value_rows):
    return lax.optimization_barrier(value_rows.astype(jnp.bfloat16)).astype(jnp.float32)


def rmsnorm(value_rows, gain):
    return (
        value_rows
        * lax.rsqrt(jnp.mean(value_rows * value_rows, axis=-1, keepdims=True) + EPSILON)
        * gain
    )


def rotary_apply(value_rows, loss_places):
    half = value_rows.shape[-1] // 2
    freqs = THETA ** (-jnp.arange(half, dtype=jnp.float32) * 2.0 / value_rows.shape[-1])
    angles = loss_places.astype(jnp.float32)[:, None] * freqs[None, :]
    cosine = jnp.cos(angles)[:, None, :]
    sine = jnp.sin(angles)[:, None, :]
    first, second = (value_rows[..., :half], value_rows[..., half:])
    return jnp.concatenate(
        [first * cosine - second * sine, first * sine + second * cosine], axis=-1
    )


def adamw(weight, grad, drift, power, rate, decay):
    moment = BETA_ONE * drift + (1.0 - BETA_ONE) * grad
    square = BETA_TWO * power + (1.0 - BETA_TWO) * grad * grad
    mean_hat = moment / (1.0 - BETA_ONE**STEP)
    square_hat = square / (1.0 - BETA_TWO**STEP)
    fresh = weight - rate * (mean_hat / (jnp.sqrt(square_hat) + ADAM_EPSILON) + decay * weight)
    return (fresh, moment, square)


def split_heads(query_rows, packed_rows):
    row_count_total = query_rows.shape[0]
    key_count_total = packed_rows.shape[0]
    query_group = QUERY_HEADS // KEY_VALUE_HEADS
    query_heads = query_rows.reshape(
        row_count_total, KEY_VALUE_HEADS, query_group, HEAD_SIZE
    ).transpose(1, 2, 0, 3)
    key_heads = (
        packed_rows[:, : KEY_VALUE_HEADS * HEAD_SIZE]
        .reshape(key_count_total, KEY_VALUE_HEADS, HEAD_SIZE)
        .transpose(1, 0, 2)
    )
    value_heads = (
        packed_rows[:, KEY_VALUE_HEADS * HEAD_SIZE :]
        .reshape(key_count_total, KEY_VALUE_HEADS, HEAD_SIZE)
        .transpose(1, 0, 2)
    )
    return (query_heads, key_heads, value_heads)


def head_scores(query_h, key_h, allowed):
    scores = jnp.einsum(
        "grd,kd->grk", query_h, key_h, preferred_element_type=jnp.float32
    ) * HEAD_SIZE ** (-0.5)
    return jnp.where(allowed[None], scores, MASKED)


def attention_forward(query_rows, packed_rows, allowed):
    row_count_total = query_rows.shape[0]
    query_heads, key_heads, value_heads = split_heads(query_rows, packed_rows)

    def one_head(item):
        query_h, key_h, value_h = item
        scores = head_scores(query_h, key_h, allowed)
        top = jnp.max(scores, axis=-1, keepdims=True)
        log_total = top + jnp.log(jnp.sum(jnp.exp(scores - top), axis=-1, keepdims=True))
        chances = jnp.exp(scores - log_total).astype(jnp.bfloat16)
        mixed = jnp.einsum("grk,kd->grd", chances, value_h, preferred_element_type=jnp.float32)
        return (mixed, log_total)

    mixed, log_total = lax.map(one_head, (query_heads, key_heads, value_heads))
    return (
        mixed.transpose(2, 0, 1, 3).reshape(row_count_total, QUERY_HEADS * HEAD_SIZE),
        log_total,
    )


def attention_backward(query_rows, packed_rows, allowed, log_total, attended_gradient):
    row_count_total = query_rows.shape[0]
    key_count_total = packed_rows.shape[0]
    query_group = QUERY_HEADS // KEY_VALUE_HEADS
    query_heads, key_heads, value_heads = split_heads(query_rows, packed_rows)
    grouped_heads = attended_gradient.reshape(
        row_count_total, KEY_VALUE_HEADS, query_group, HEAD_SIZE
    ).transpose(1, 2, 0, 3)

    def one_head(item):
        query_h, key_h, value_h, total_h, grad_h = item
        chances = jnp.exp(head_scores(query_h, key_h, allowed) - total_h)
        chances_low = chances.astype(jnp.bfloat16)
        grad_chances = rounded(
            jnp.einsum("grd,kd->grk", grad_h, value_h, preferred_element_type=jnp.float32)
        )
        grad_scores = chances * (
            grad_chances - jnp.sum(chances * grad_chances, axis=-1, keepdims=True)
        )
        grad_scores = grad_scores.astype(jnp.bfloat16)
        grad_query = jnp.einsum(
            "grk,kd->grd", grad_scores, key_h, preferred_element_type=jnp.float32
        ) * HEAD_SIZE ** (-0.5)
        key_gradient = jnp.einsum(
            "grk,grd->kd", grad_scores, query_h, preferred_element_type=jnp.float32
        ) * HEAD_SIZE ** (-0.5)
        value_gradient = jnp.einsum(
            "grk,grd->kd", chances_low, grad_h, preferred_element_type=jnp.float32
        )
        return (grad_query, key_gradient, value_gradient)

    grad_query, key_gradient, value_gradient = lax.map(
        one_head, (query_heads, key_heads, value_heads, log_total, grouped_heads)
    )
    grad_query = grad_query.transpose(2, 0, 1, 3).reshape(row_count_total, QUERY_HEADS, HEAD_SIZE)
    key_gradient = key_gradient.transpose(1, 0, 2).reshape(
        key_count_total, KEY_VALUE_HEADS * HEAD_SIZE
    )
    value_gradient = value_gradient.transpose(1, 0, 2).reshape(
        key_count_total, KEY_VALUE_HEADS * HEAD_SIZE
    )
    return (grad_query, jnp.concatenate([key_gradient, value_gradient], axis=1))


def layer_weights(full, number):
    incoming, outgoing, expand, contract, scales = full
    return (
        incoming[number],
        outgoing[number],
        expand[number],
        contract[number],
        scales[2 * number],
        scales[2 * number + 1],
    )


def layer_forward(residual, weights, loss_places, allowed):
    incoming, outgoing, expand, contract, gain_attn, gain_ffn = weights
    row_count_total = residual.shape[0]
    query_width = QUERY_HEADS * HEAD_SIZE
    key_width = KEY_VALUE_HEADS * HEAD_SIZE
    normed = rmsnorm(residual, gain_attn.astype(jnp.float32)).astype(jnp.bfloat16)
    joined_heads = matmul(normed, incoming)
    query_rows = rotary_apply(
        joined_heads[:, :query_width].reshape(row_count_total, QUERY_HEADS, HEAD_SIZE), loss_places
    ).astype(jnp.bfloat16)
    key_collection = rotary_apply(
        joined_heads[:, query_width : query_width + key_width].reshape(
            row_count_total, KEY_VALUE_HEADS, HEAD_SIZE
        ),
        loss_places,
    )
    key_collection = key_collection.astype(jnp.bfloat16).reshape(row_count_total, key_width)
    value_collection = joined_heads[:, query_width + key_width :].astype(jnp.bfloat16)
    packed_rows = jnp.concatenate([key_collection, value_collection], axis=1)
    gathered = lax.all_gather(packed_rows, ("context", "tensor"), axis=0, tiled=True)
    mixed, log_total = attention_forward(query_rows, gathered, allowed)
    attended = mixed.astype(jnp.bfloat16)
    middle = residual + matmul(attended, outgoing)
    normed_ffn = rmsnorm(middle, gain_ffn.astype(jnp.float32)).astype(jnp.bfloat16)
    gate_up = matmul(normed_ffn, expand)
    hidden = (jax.nn.silu(gate_up[:, :FF]) * gate_up[:, FF:]).astype(jnp.bfloat16)
    result = middle + matmul(hidden, contract)
    return (result, (residual, middle, query_rows, gathered, log_total, attended))


def activate(both):
    return jax.nn.silu(both[:, :FF]) * both[:, FF:]


def layer_backward(grad_residual, weights, saved, loss_places, allowed):
    incoming, outgoing, expand, contract, gain_attn, gain_ffn = weights
    residual, middle, query_rows, gathered, log_total, attended = saved
    row_count_total = residual.shape[0]
    query_width = QUERY_HEADS * HEAD_SIZE
    key_width = KEY_VALUE_HEADS * HEAD_SIZE
    normed_ffn, ffn_pull = jax.vjp(rmsnorm, middle, gain_ffn.astype(jnp.float32))
    normed_low = normed_ffn.astype(jnp.bfloat16)
    hidden, act_pull = jax.vjp(activate, matmul(normed_low, expand))
    hidden_low = hidden.astype(jnp.bfloat16)
    branch = grad_residual.astype(jnp.bfloat16)
    grad_contract = across(hidden_low, branch)
    grad_hidden = rounded(against(branch, contract))
    grad_gate_up = act_pull(grad_hidden)[0].astype(jnp.bfloat16)
    grad_expand = across(normed_low, grad_gate_up)
    grad_normed = rounded(against(grad_gate_up, expand))
    grad_middle, grad_gain_ffn = ffn_pull(grad_normed)
    grad_middle = grad_middle + grad_residual
    branch = grad_middle.astype(jnp.bfloat16)
    grad_outgoing = across(attended, branch)
    attended_gradient = against(branch, outgoing).astype(jnp.bfloat16)
    grad_queries, grad_packed = attention_backward(
        query_rows, gathered, allowed, log_total, attended_gradient
    )
    local_gradient = lax.psum_scatter(
        grad_packed, ("context", "tensor"), scatter_dimension=0, tiled=True
    )
    normed_attn, attn_pull = jax.vjp(rmsnorm, residual, gain_attn.astype(jnp.float32))
    normed_low = normed_attn.astype(jnp.bfloat16)
    _, rope_queries = jax.vjp(
        lambda value_rows: rotary_apply(value_rows, loss_places),
        jnp.zeros((row_count_total, QUERY_HEADS, HEAD_SIZE), jnp.float32),
    )
    _, rotary_keys = jax.vjp(
        lambda value_rows: rotary_apply(value_rows, loss_places),
        jnp.zeros((row_count_total, KEY_VALUE_HEADS, HEAD_SIZE), jnp.float32),
    )
    grad_q = rope_queries(grad_queries)[0].reshape(row_count_total, query_width)
    key_heads_gradient = rotary_keys(
        local_gradient[:, :key_width].reshape(row_count_total, KEY_VALUE_HEADS, HEAD_SIZE)
    )[0].reshape(row_count_total, key_width)
    grad_joined = jnp.concatenate(
        [grad_q, key_heads_gradient, local_gradient[:, key_width:]], axis=1
    ).astype(jnp.bfloat16)
    grad_incoming = across(normed_low, grad_joined)
    grad_normed = rounded(against(grad_joined, incoming))
    grad_input, grad_gain_attn = attn_pull(grad_normed)
    grads = (
        grad_incoming,
        grad_outgoing,
        grad_expand,
        grad_contract,
        grad_gain_attn,
        grad_gain_ffn,
    )
    return (grad_input + grad_middle, grads)


def combine(earlier, later):
    top_a, total_a, target_a = earlier
    top_b, total_b, target_b = later
    top = jnp.maximum(top_a, top_b)
    return (
        top,
        total_a * jnp.exp(top_a - top) + total_b * jnp.exp(top_b - top),
        target_a + target_b,
    )


def on_device(
    tokens,
    lengths,
    loss_positions,
    teacher_ids,
    label_ids,
    embedding,
    incoming,
    outgoing,
    expand,
    contract,
    scales,
    drift_embedding,
    incoming_first_moment,
    drift_outgoing,
    drift_expand,
    drift_contract,
    drift_scales,
    power_embedding,
    incoming_second_moment,
    power_outgoing,
    power_expand,
    power_contract,
    power_scales,
):
    ranks = lax.axis_size(("context", "tensor"))
    seq_rank = lax.axis_index(("context", "tensor"))
    full_len = tokens.shape[2]
    row_count_total = full_len // ranks
    first_row = seq_rank * row_count_total
    vocab_rows = embedding.shape[0]
    vocab_start = seq_rank * vocab_rows
    batches = tokens.shape[0]
    positions_count = loss_positions.shape[2]
    count_all = batches * lax.axis_size("fsdp") * positions_count
    table = embedding.astype(jnp.bfloat16)
    masters = (incoming, outgoing, expand, contract, scales)
    lowered = tuple((master.astype(jnp.bfloat16) for master in masters))
    loss_places = first_row + jnp.arange(row_count_total, dtype=jnp.int32)
    keyplace = jnp.arange(full_len, dtype=jnp.int32)
    position_index = jnp.arange(positions_count, dtype=jnp.int32)
    layer_sums = tuple((jnp.zeros(master.shape, jnp.float32) for master in masters))
    table_grad = jnp.zeros(embedding.shape, jnp.float32)
    loss_sum = jnp.zeros((), jnp.float32)
    for batch_number in range(batches):
        full = jax.tree.map(
            lambda part, own: part.astype(own.dtype),
            lax.all_gather(shortened(lowered), ("fsdp", "tensor"), axis=1, tiled=True),
            lowered,
        )
        token_row = tokens[batch_number, 0]
        length = lengths[batch_number, 0]
        allowed = (keyplace[None, :] <= loss_places[:, None]) & (keyplace[None, :] < length)
        local_ids = token_row - vocab_start
        inside = (local_ids >= 0) & (local_ids < vocab_rows)
        found = jnp.take(table, jnp.where(inside, local_ids, 0), axis=0)
        residual = lax.psum_scatter(
            jnp.where(inside[:, None], found, jnp.zeros((), jnp.bfloat16))
            .astype(jnp.float32)
            .astype(jnp.bfloat16),
            ("context", "tensor"),
            scatter_dimension=0,
            tiled=True,
        ).astype(jnp.float32)
        number = 0
        residual, saved = layer_forward(residual, layer_weights(full, number), loss_places, allowed)
        saves = [saved]
        final, final_pull = jax.vjp(rmsnorm, residual, full[4][2 * LAYER_COUNT].astype(jnp.float32))
        final_low = final.astype(jnp.bfloat16)
        spots = loss_positions[batch_number, 0] % length
        picker = (spots[:, None] == loss_places[None, :]).astype(jnp.bfloat16)
        chosen = lax.psum(matmul(picker, final_low).astype(jnp.bfloat16), ("context", "tensor"))
        logits = against(chosen, table)
        teacher = teacher_ids[batch_number, 0]
        labels = label_ids[batch_number, 0]
        teacher_local = teacher - vocab_start
        teacher_inside = (teacher_local >= 0) & (teacher_local < vocab_rows)
        label_local = labels - vocab_start
        label_inside = (label_local >= 0) & (label_local < vocab_rows)
        teacher_vals = jnp.take_along_axis(
            logits, jnp.where(teacher_inside, teacher_local, 0), axis=1
        )
        label_vals = jnp.take_along_axis(
            logits, jnp.where(label_inside, label_local, 0)[:, None], axis=1
        )[:, 0]
        target_part = jnp.sum(jnp.where(teacher_inside, teacher_vals, 0.0), axis=1) / TEACH
        target_part = target_part + jnp.where(label_inside, label_vals, 0.0)
        top = jnp.max(logits, axis=1)
        total = jnp.sum(jnp.exp(logits - top[:, None]), axis=1)
        top, total, target = merged((top, total, target_part), ("context", "tensor"), combine)
        log_total = top + jnp.log(total)
        counts = jnp.sum((teacher[:, :, None] == teacher[:, None, :]).astype(jnp.float32), axis=-1)
        entropy_part = jnp.mean(jnp.log(counts / TEACH), axis=1)
        loss_sum = loss_sum + jnp.sum(entropy_part + 2.0 * log_total - target)
        chances = jnp.exp(logits - log_total[:, None])
        frequencies = jnp.zeros((positions_count, vocab_rows + 1), jnp.float32)
        frequencies = frequencies.at[
            position_index[:, None], jnp.where(teacher_inside, teacher_local, vocab_rows)
        ].add(1.0 / TEACH)
        frequencies = frequencies.at[
            position_index, jnp.where(label_inside, label_local, vocab_rows)
        ].add(1.0)
        grad_logits = ((2.0 * chances - frequencies[:, :vocab_rows]) / count_all).astype(
            jnp.bfloat16
        )
        table_grad = table_grad + across(grad_logits, chosen)
        grad_chosen = lax.psum(matmul(grad_logits, table), ("context", "tensor"))
        grad_final = rounded(
            jnp.dot(picker.astype(jnp.float32).T, grad_chosen, precision=lax.Precision.HIGHEST)
        )
        grad_residual, grad_final_gain = final_pull(grad_final)
        full = jax.tree.map(
            lambda part, own: part.astype(own.dtype),
            lax.all_gather(shortened(lowered), ("fsdp", "tensor"), axis=1, tiled=True),
            lowered,
        )
        layer_grads = [None] * LAYER_COUNT
        for number in reversed(range(LAYER_COUNT)):
            grad_residual, layer_grads[number] = layer_backward(
                grad_residual, layer_weights(full, number), saves[number], loss_places, allowed
            )
        grad_tokens = lax.all_gather(
            grad_residual.astype(jnp.bfloat16), ("context", "tensor"), axis=0, tiled=True
        )
        token_local = token_row - vocab_start
        token_inside = (token_local >= 0) & (token_local < vocab_rows)
        slots = jnp.where(token_inside, token_local, vocab_rows)
        table_grad = (
            table_grad
            + jax.ops.segment_sum(
                grad_tokens.astype(jnp.float32), slots, num_segments=vocab_rows + 1
            )[:vocab_rows]
        )
        gain_rows = [grads[kind] for grads in layer_grads for kind in (4, 5)] + [grad_final_gain]
        stacked = (
            jnp.stack([grads[0] for grads in layer_grads]),
            jnp.stack([grads[1] for grads in layer_grads]),
            jnp.stack([grads[2] for grads in layer_grads]),
            jnp.stack([grads[3] for grads in layer_grads]),
            jnp.stack(gain_rows),
        )
        reduced = (
            lax.psum_scatter(stacked[0], ("fsdp", "tensor"), scatter_dimension=1, tiled=True),
            lax.psum_scatter(stacked[1], ("fsdp", "tensor"), scatter_dimension=1, tiled=True),
            lax.psum_scatter(stacked[2], ("fsdp", "tensor"), scatter_dimension=1, tiled=True),
            lax.psum_scatter(stacked[3], ("fsdp", "tensor"), scatter_dimension=1, tiled=True),
            lax.psum_scatter(stacked[4], ("fsdp", "tensor"), scatter_dimension=1, tiled=True),
        )
        layer_sums = tuple((held + added for held, added in zip(layer_sums, reduced)))
    layer_totals = lax.psum(layer_sums, "context")
    table_total = lax.psum(table_grad, "fsdp")
    lead_context = (lax.axis_index("context") == 0).astype(jnp.float32)
    lead_fsdp = (lax.axis_index("fsdp") == 0).astype(jnp.float32)
    lead_seq = (seq_rank == 0).astype(jnp.float32)
    layer_square = sum((jnp.sum(grad * grad) for grad in layer_totals))
    square_total, loss_total = lax.psum(
        (
            lead_context * layer_square + lead_fsdp * jnp.sum(table_total * table_total),
            lead_seq * loss_sum,
        ),
        ("fsdp", "context", "tensor"),
    )
    grad_norm = jnp.sqrt(square_total)
    loss_value = loss_total / count_all
    factor = CLIP / jnp.maximum(grad_norm, CLIP)
    weights = (embedding, incoming, outgoing, expand, contract, scales)
    grads = (table_total,) + tuple(layer_totals)
    drifts = (
        drift_embedding,
        incoming_first_moment,
        drift_outgoing,
        drift_expand,
        drift_contract,
        drift_scales,
    )
    powers = (
        power_embedding,
        incoming_second_moment,
        power_outgoing,
        power_expand,
        power_contract,
        power_scales,
    )
    rates = (RATE_MATRIX, RATE_MATRIX, RATE_MATRIX, RATE_MATRIX, RATE_MATRIX, RATE_GAIN)
    decays = (DECAY, DECAY, DECAY, DECAY, DECAY, 0.0)
    updated = [
        adamw(
            weights[index],
            grads[index] * factor,
            drifts[index],
            powers[index],
            rates[index],
            decays[index],
        )
        for index in range(6)
    ]
    return (
        loss_value,
        grad_norm,
        updated[0][0],
        updated[1][0],
        updated[2][0],
        updated[3][0],
        updated[4][0],
        updated[5][0],
        updated[0][1],
        updated[1][1],
        updated[2][1],
        updated[3][1],
        updated[4][1],
        updated[5][1],
        updated[0][2],
        updated[1][2],
        updated[2][2],
        updated[3][2],
        updated[4][2],
        updated[5][2],
    )


def solution(mesh):
    in_specs = (
        P(None, "fsdp", None),
        P(None, "fsdp"),
        P(None, "fsdp", None),
        P(None, "fsdp", None, None),
        P(None, "fsdp", None),
        P(("context", "tensor"), None),
        P(None, ("fsdp", "tensor"), None),
        P(None, ("fsdp", "tensor"), None),
        P(None, ("fsdp", "tensor"), None),
        P(None, ("fsdp", "tensor"), None),
        P(None, ("fsdp", "tensor")),
        P(("context", "tensor"), None),
        P(None, ("fsdp", "tensor"), None),
        P(None, ("fsdp", "tensor"), None),
        P(None, ("fsdp", "tensor"), None),
        P(None, ("fsdp", "tensor"), None),
        P(None, ("fsdp", "tensor")),
        P(("context", "tensor"), None),
        P(None, ("fsdp", "tensor"), None),
        P(None, ("fsdp", "tensor"), None),
        P(None, ("fsdp", "tensor"), None),
        P(None, ("fsdp", "tensor"), None),
        P(None, ("fsdp", "tensor")),
    )
    out_specs = (
        P(),
        P(),
        P(("context", "tensor"), None),
        P(None, ("fsdp", "tensor"), None),
        P(None, ("fsdp", "tensor"), None),
        P(None, ("fsdp", "tensor"), None),
        P(None, ("fsdp", "tensor"), None),
        P(None, ("fsdp", "tensor")),
        P(("context", "tensor"), None),
        P(None, ("fsdp", "tensor"), None),
        P(None, ("fsdp", "tensor"), None),
        P(None, ("fsdp", "tensor"), None),
        P(None, ("fsdp", "tensor"), None),
        P(None, ("fsdp", "tensor")),
        P(("context", "tensor"), None),
        P(None, ("fsdp", "tensor"), None),
        P(None, ("fsdp", "tensor"), None),
        P(None, ("fsdp", "tensor"), None),
        P(None, ("fsdp", "tensor"), None),
        P(None, ("fsdp", "tensor")),
    )
    return jax.shard_map(
        on_device, mesh=mesh, in_specs=in_specs, out_specs=out_specs, check_vma=False
    )
```

profile of v0, /device:TPU:0, one launch (start us, length us, event | category | flops | bytes accessed | tf_op | source)
XLA Modules:
  0.0 3513.9 jit_solution(15593453950234156245)
XLA Ops:
  86.4 43.9 %reduce-scatter.32.cloned.1.call-done = bf16[128,960]{1,0:T(8,128)(2,1)} async-done(((bf16[1024,960]{1,0:T(8,128)(2,1)}), bf16[128,960]{1,0:T(8,128)(2,1)}) %reduce-scatter.32.cloned.1.call-update) | async-done | bytes 245776
  131.5 43.8 %reduce-scatter.30.cloned.1.call-done = bf16[128,960]{1,0:T(8,128)(2,1)} async-done(((bf16[1024,960]{1,0:T(8,128)(2,1)}), bf16[128,960]{1,0:T(8,128)(2,1)}) %reduce-scatter.30.cloned.1.call-update) | async-done | bytes 245776
  271.1 22.3 all-gather.39.cloned.1.call-done
  316.5 73.2 %all-gather.33.cloned.1.call-done = bf16[1,960,5120]{2,1,0:T(8,128)(2,1)} async-done(((bf16[1,120,5120]{2,1,0:T(8,128)(2,1)}), bf16[1,960,5120]{2,1,0:T(8,128)(2,1)}) %all-gather.33.cloned.1.call-update) | async-done | bytes 9830416 | tf_op jit(solution)/shard_map/all_gather | solution.py:348
  397.0 49.3 %all-gather.35.cloned.1.call-done = bf16[1,2560,960]{2,1,0:T(8,128)(2,1)} async-done(((bf16[1,320,960]{2,1,0:T(8,128)(2,1)}), bf16[1,2560,960]{2,1,0:T(8,128)(2,1)}) %all-gather.35.cloned.1.call-update) | async-done | bytes 4915216 | tf_op jit(solution)/shard_map/all_gather | solution.py:348
  467.5 48.9 %scatter_custom_fusion.7 = f32[786560]{0:T(1024)} fusion(s32[8192]{0:T(1024)S(1)} %reshape.1249, f32[8192]{0:T(1024)S(1)} %broadcast.1338, f32[]{:T(128)} %constant.457.clone.1), kind=kCustom, calls=%fused_computation.330 | custom fusion | flops 8192 | bytes 3146244
  540.3 48.8 %scatter_custom_fusion.8 = f32[786560]{0:T(1024)} fusion(s32[8192]{0:T(1024)S(1)} %reshape.1255, f32[8192]{0:T(1024)S(1)} %broadcast.1338, f32[]{:T(128)} %constant.457.clone.1), kind=kCustom, calls=%fused_computation.328 | custom fusion | flops 8192 | bytes 3146244
  613.3 49.1 %scatter_custom_fusion.6 = f32[786560]{0:T(1024)} fusion(s32[8192]{0:T(1024)S(1)} %reshape.1243, f32[8192]{0:T(1024)S(1)} %broadcast.1338, f32[]{:T(128)} %constant.457.clone.1), kind=kCustom, calls=%fused_computation.332 | custom fusion | flops 8192 | bytes 3146244
  697.4 65.1 %gather_fusion.1 = f32[8192]{0:T(1024)S(1)} fusion(f32[128,6144]{1,0:T(8,128)S(1)} %get-tuple-element.1451, s32[8192]{0:T(1024)S(1)} %reshape.1346), kind=kCustom, calls=%fused_computation.1.clone | custom fusion | bytes 131072 | tf_op jit(solution)/shard_map/jit(take_along_axis)/gather | solution.py:380
  763.1 23.5 all-gather.8
  807.6 319.6 %gather_fusion.4 = f32[8192]{0:T(1024)S(1)} fusion(f32[128,6144]{1,0:T(8,128)} %get-tuple-element.1453, s32[8192]{0:T(1024)S(1)} %reshape.1359), kind=kCustom, calls=%fused_computation.5.clone | custom fusion | bytes 131072 | tf_op jit(solution)/shard_map/jit(take_along_axis)/gather | solution.py:380
  1129.7 41.5 %all-gather.11 = f32[8,1,128]{2,1,0:T(1,128)S(1)} all-gather(f32[1,1,128]{2,1,0:T(1,128)S(1)} %bitcast.1045), channel_id=5, replica_groups=mesh['fsdp'=4,'context'=4,'tensor'=2] {'context','tensor'}, dimensions={0}, use_global_device_ids=true | all-gather | bytes 4608 | tf_op jit(solution)/shard_map/all_gather | solution.py:36
  1192.3 303.9 %gather_fusion.7 = f32[8192]{0:T(1024)S(1)} fusion(f32[128,6144]{1,0:T(8,128)} %get-tuple-element.1455, s32[8192]{0:T(1024)S(1)} %reshape.1372), kind=kCustom, calls=%fused_computation.6.clone | custom fusion | bytes 131072 | tf_op jit(solution)/shard_map/jit(take_along_axis)/gather | solution.py:380
  1498.6 40.8 %all-gather.14 = f32[8,1,128]{2,1,0:T(1,128)S(1)} all-gather(f32[1,1,128]{2,1,0:T(1,128)S(1)} %bitcast.1046), channel_id=7, replica_groups=mesh['fsdp'=4,'context'=4,'tensor'=2] {'context','tensor'}, dimensions={0}, use_global_device_ids=true | all-gather | bytes 4608 | tf_op jit(solution)/shard_map/all_gather | solution.py:36
  1608.5 58.3 %all-reduce.35.cloned.1.call-done = (f32[128,960]{0,1:T(8,128)}, f32[128,960]{0,1:T(8,128)}, f32[128,960]{0,1:T(8,128)}) async-done(((f32[128,960]{0,1:T(8,128)}, f32[128,960]{0,1:T(8,128)}, f32[128,960]{0,1:T(8,128)}), (f32[128,960]{0,1:T(8,128)}, f32[128,960]{0,1:T(8,128)}, f32[128,960]{0,1:T(8,128)})) %all-reduce.35.cloned.1.call-update) | async-done | bytes 1474576 | tf_op jit(solution)/shard_map/psum | solution.py:407
  1706.0 48.0 %while.148 = (s32[]{:T(128)}, f32[5,3,128,64]{2,3,1,0:T(8,128)}, f32[5,1024,64]{1,2,0:T(8,128)}, f32[5,1024,64]{1,2,0:T(8,128)}, bf16[5,3,128,64]{2,3,1,0:T(8,12...) while((s32[]{:T(128)}, f32[5,3,128,64]{2,3,1,0:T(8,128)}, ...), condition=%wide.region_69.73_spmd.clone, body=%wide.region_67.72_spmd.clone.sunk | while | flops 256728704 | bytes 10926209 | solution.py:173
  1763.9 44.7 %while.147 = (s32[]{:T(128)}, f32[5,3,128,64]{2,3,1,0:T(8,128)}, f32[5,1024,64]{1,2,0:T(8,128)}, f32[5,1024,64]{1,2,0:T(8,128)S(1)}, bf16[5,3,128,64]{2,3,1,0:T(...) while((s32[]{:T(128)}, f32[5,3,128,64]{2,3,1,0:T(8,128)}, ...), condition=%wide.region_59.63_spmd.clone, body=%wide.region_57.62_spmd.clone.sunk | while | flops 256728704 | bytes 10926209 | solution.py:173
  1814.5 37.1 %while.149 = (s32[]{:T(128)}, f32[5,3,128,64]{2,3,1,0:T(8,128)}, f32[5,1024,64]{1,2,0:T(8,128)S(1)}, f32[5,1024,64]{1,2,0:T(8,128)S(1)}, bf16[5,3,128,64]{2,3,1,...) while((s32[]{:T(128)}, f32[5,3,128,64]{2,3,1,0:T(8,128)}, ...), condition=%wide.region_79.83_spmd.clone, body=%wide.region_77.82_spmd.clone.sunk | while | flops 256728704 | bytes 10926209 | solution.py:173
  1859.6 42.5 %reduce-scatter.24.cloned.1.call-done = f32[128,640]{0,1:T(8,128)} async-done(((f32[1024,640]{0,1:T(8,128)}), f32[128,640]{0,1:T(8,128)}) %reduce-scatter.24.cloned.1.call-update) | async-done | bytes 327696 | tf_op jit(solution)/shard_map/reduce_scatter | solution.py:256
  1923.3 22.2 copy.166
  1978.4 21.9 add_bitcast_fusion
  2065.6 24.2 copy.190
  2093.8 20.8 scatter_custom_fusion.4
  2132.5 24.1 copy.191
  2198.9 24.3 copy.192
  2223.2 46.5 %add_add_fusion = f32[6144,960]{0,1:T(8,128)} fusion(f32[6144,960]{0,1:T(8,128)} %copy.192, f32[6144,960]{0,1:T(8,128)} %copy.191, f32[6144,960]{0,1:T(8,128)} %fusion.470, f32[6144,960]{0,1:T(8,128)} %fusion.469, f32[6144,960]{0,1:T(8,128)} %copy.190, bf16[128,960]{0,1:T(8,128)(2,1)S(1)} %copy-done.112, bf16[128,6144]{1,0:T(8,128)(2,1)S(1)} %copy-done.36), kind=kOutput, calls=%fused_computation.233 | convolution fusion | flops 1539440640 | bytes 143376384 | tf_op jit(solution)/shard_map/dot_general | solution.py:51
  2281.5 196.1 %reduce-scatter.28.cloned.1.call-done = f32[1,120,5120]{2,1,0:T(8,128)} async-done(((f32[1,960,5120]{2,1,0:T(8,128)}), f32[1,120,5120]{2,1,0:T(8,128)}) %reduce-scatter.28.cloned.1.call-update) | async-done | bytes 2457616 | tf_op jit(solution)/shard_map/reduce_scatter | solution.py:445
  2480.4 27.8 all-reduce.20
  2518.9 742.0 %all-reduce.31.cloned.1.call-done = f32[6144,960]{0,1:T(8,128)} async-done(((f32[6144,960]{0,1:T(8,128)}), f32[6144,960]{0,1:T(8,128)}) %all-reduce.31.cloned.1.call-update) | async-done | bytes 23592976 | tf_op jit(solution)/shard_map/psum | solution.py:451
  3274.0 108.0 %all-reduce.37.cloned.1.call-done = (f32[1,120,1600]{2,1,0:T(8,128)}, f32[1,120,960]{2,1,0:T(8,128)}, f32[1,120,5120]{2,1,0:T(8,128)}, f32[1,320,960]{2,1,0:T(8,128)}) async-done(((f32[1,120,1600]{2,1,0:T(8,128)}, f32[1,120,960]{2,1,0:T(8,128)}, f32[1,120,5120]{2,1,0:T(8,128)}, f32[1,320,960]{2,1,0:T(8,128)}), (f32[1,120,1600]{2,1,0:T(8,128)}, f32[1,120,960]{2,1,0:T(8,128)}, f32[1,120,5120]{2,1,0:T(8,128)}, ...) | async-done | bytes 4915216 | tf_op jit(solution)/shard_map/psum | solution.py:450
  3392.1 39.9 %all-reduce.21 = (f32[]{:T(128)}, f32[]{:T(128)}) all-reduce(f32[]{:T(128)S(6)} %mul.1490, f32[]{:T(128)S(6)} %add.941), channel_id=1, replica_groups=mesh['fsdp'=4,'context'=4,'tensor'=2] {'fsdp','context','tensor'}, use_global_device_ids=true, to_apply=%region_51.55 | all-reduce | flops 2 | bytes 16 | tf_op jit(solution)/shard_map/psum | solution.py:456
  3448.4 55.9 %multiply_subtract_fusion = (f32[6144,960]{0,1:T(8,128)}, f32[6144,960]{0,1:T(8,128)}, f32[6144,960]{0,1:T(8,128)}) fusion(f32[6144,960]{0,1:T(8,128)} %param.52, f32[6144,960]{0,1:T(8,128)} %all-reduce.31.cloned.1.call-done, f32[]{:T(128)S(6)} %div.330, f32[6144,960]{0,1:T(8,128)} %param.58, f32[6144,960]{0,1:T(8,128)} %param.64), kind=kLoop, calls=%fused_computation.230 | loop fusion | flops 94371840 | bytes 165150720 | tf_op jit(solution)/shard_map/sub | solution.py:91
  (1057 shorter events, 884.2 us)
Async XLA Ops:
  8.0 77.3 %reduce-scatter.34.cloned.1.call-start = ((), (), s32[]{:S(2)}) async-start(), calls=%async_computation.27 | async-start | bytes 2359296
  41.3 89.1 %reduce-scatter.32.cloned.1.call-start = ((), (), s32[]{:S(2)}) async-start(), calls=%async_computation.26 | async-start | bytes 2359296
  54.3 121.0 %reduce-scatter.30.cloned.1.call-start = ((), (), s32[]{:S(2)}) async-start(), calls=%async_computation.25 | async-start | bytes 2359296
  67.7 109.3 %all-gather.27.cloned.1.call-start = ((), (), s32[]{:S(2)}) async-start(), calls=%async_computation.9 | async-start | bytes 3594240 | tf_op jit(solution)/shard_map/all_gather | solution.py:348
  68.6 141.2 %all-gather.37.cloned.1.call-start = ((), (), s32[]{:S(2)}) async-start(), calls=%async_computation.14 | async-start | bytes 1474560 | tf_op jit(solution)/shard_map/all_gather | solution.py:217
  82.3 100.1 %copy-start.122 = (f32[1,960]{1,0:T(1,128)}, f32[1,960]{1,0:T(1,128)S(1)}, u32[]{:S(2)}) copy-start(f32[1,960]{1,0:T(1,128)S(1)} %get-tuple-element.1403) | copy-start | bytes 11524
  82.5 101.6 %copy-start.132 = (f32[128,32]{0,1:T(8,128)}, f32[128,32]{0,1:T(8,128)S(1)}, u32[]{:S(2)}) copy-start(f32[128,32]{0,1:T(8,128)S(1)} %get-tuple-element.1431) | copy-start | bytes 49156
  82.5 125.4 %copy-start.130 = (f32[128,32]{0,1:T(8,128)}, f32[128,32]{0,1:T(8,128)S(1)}, u32[]{:S(2)}) copy-start(f32[128,32]{0,1:T(8,128)S(1)} %get-tuple-element.1430) | copy-start | bytes 49156
  86.4 94.3 %copy-start.43 = (bf16[128,960]{0,1:T(8,128)(2,1)}, bf16[128,960]{0,1:T(8,128)(2,1)S(1)}, u32[]{:S(2)}) copy-start(bf16[128,960]{0,1:T(8,128)(2,1)S(1)} %copy.179) | copy-start | bytes 737284
  131.5 138.2 %copy-start.30 = (bf16[128,960]{0,1:T(8,128)(2,1)}, bf16[128,960]{0,1:T(8,128)(2,1)S(1)}, u32[]{:S(2)}) copy-start(bf16[128,960]{0,1:T(8,128)(2,1)S(1)} %copy.177) | copy-start | bytes 737284
  184.9 51.8 %all-gather.29.cloned.1.call-start = ((), (), s32[]{:S(2)}) async-start(), calls=%async_computation.10 | async-start | bytes 1474560 | tf_op jit(solution)/shard_map/all_gather | solution.py:217
  185.7 81.3 %all-gather.31.cloned.1.call-start = ((), (), s32[]{:S(2)}) async-start(), calls=%async_computation.11 | async-start | bytes 2211840 | tf_op jit(solution)/shard_map/all_gather | solution.py:348
  186.5 106.9 %all-gather.39.cloned.1.call-start = ((), (), s32[]{:S(2)}) async-start(), calls=%async_computation.15 | async-start | bytes 1474560 | tf_op jit(solution)/shard_map/all_gather | solution.py:217
  187.3 202.3 %all-gather.33.cloned.1.call-start = ((), (), s32[]{:S(2)}) async-start(), calls=%async_computation.12 | async-start | bytes 11059200 | tf_op jit(solution)/shard_map/all_gather | solution.py:348
  190.4 255.9 %all-gather.35.cloned.1.call-start = ((), (), s32[]{:S(2)}) async-start(), calls=%async_computation.13 | async-start | bytes 5898240 | tf_op jit(solution)/shard_map/all_gather | solution.py:348
  191.4 495.5 %all-reduce.39.cloned.1.call-start = ((), (), s32[]{:S(2)}) async-start(), calls=%async_computation.32 | async-start | bytes 1474560 | tf_op jit(solution)/shard_map/psum | solution.py:372
  269.6 191.6 %copy-start.18 = (f32[128,960]{0,1:T(8,128)}, f32[128,960]{0,1:T(8,128)S(1)}, u32[]{:S(2)}) copy-start(f32[128,960]{0,1:T(8,128)S(1)} %get-tuple-element.1439) | copy-start | bytes 1474564
  270.6 186.2 %copy-start.15 = (f32[128,960]{0,1:T(8,128)}, f32[128,960]{0,1:T(8,128)S(1)}, u32[]{:S(2)}) copy-start(f32[128,960]{0,1:T(8,128)S(1)} %get-tuple-element.1443) | copy-start | bytes 1474564
  315.9 130.3 %copy-start.6 = (f32[128,960]{0,1:T(8,128)}, f32[128,960]{0,1:T(8,128)S(1)}, u32[]{:S(2)}) copy-start(f32[128,960]{0,1:T(8,128)S(1)} %get-tuple-element.1447) | copy-start | bytes 1474564
  466.4 1200.4 %all-reduce.35.cloned.1.call-start = ((), (), s32[]{:S(2)}) async-start(), calls=%async_computation.30 | async-start | bytes 2949120 | tf_op jit(solution)/shard_map/psum | solution.py:407
  1608.0 248.4 %reduce-scatter.22.cloned.1.call-start = ((), (), s32[]{:S(2)}) async-start(), calls=%async_computation.17 | async-start | bytes 2949120 | tf_op jit(solution)/shard_map/reduce_scatter | solution.py:256
  1757.7 100.4 %reduce-scatter.20.cloned.1.call-start = ((), (), s32[]{:S(2)}) async-start(), calls=%async_computation.16 | async-start | bytes 2949120 | tf_op jit(solution)/shard_map/reduce_scatter | solution.py:256
  1811.7 90.4 %reduce-scatter.24.cloned.1.call-start = ((), (), s32[]{:S(2)}) async-start(), calls=%async_computation.18 | async-start | bytes 2949120 | tf_op jit(solution)/shard_map/reduce_scatter | solution.py:256
  1853.3 169.4 %all-gather.41.cloned.1.call-start = ((), (), s32[]{:S(2)}) async-start(), calls=%async_computation.19 | async-start | bytes 2211840 | tf_op jit(solution)/shard_map/all_gather | solution.py:422
  1913.4 176.3 %all-gather.43.cloned.1.call-start = ((), (), s32[]{:S(2)}) async-start(), calls=%async_computation.20 | async-start | bytes 2211840 | tf_op jit(solution)/shard_map/all_gather | solution.py:422
  1914.0 242.6 %all-gather.45.cloned.1.call-start = ((), (), s32[]{:S(2)}) async-start(), calls=%async_computation.21 | async-start | bytes 2211840 | tf_op jit(solution)/shard_map/all_gather | solution.py:422
  1914.7 357.0 %all-reduce.33.cloned.1.call-start = ((), (), s32[]{:S(2)}) async-start(), calls=%async_computation.28 | async-start | bytes 20971520
  1945.5 329.6 %reduce-scatter.26.cloned.1.call-start = ((), (), s32[]{:S(2)}) async-start(), calls=%async_computation.23 | async-start | bytes 4423680 | tf_op jit(solution)/shard_map/reduce_scatter | solution.py:444
  1951.1 330.4 %reduce-scatter.36.cloned.1.call-start = ((), (), s32[]{:S(2)}) async-start(), calls=%async_computation.29 | async-start | bytes 7188480
  1958.3 519.3 %reduce-scatter.28.cloned.1.call-start = ((), (), s32[]{:S(2)}) async-start(), calls=%async_computation.24 | async-start | bytes 22118400 | tf_op jit(solution)/shard_map/reduce_scatter | solution.py:445
  2000.4 1260.5 %all-reduce.31.cloned.1.call-start = ((), (), s32[]{:S(2)}) async-start(), calls=%async_computation.22 | async-start | bytes 47185920 | tf_op jit(solution)/shard_map/psum | solution.py:451
  2269.7 1112.2 %all-reduce.37.cloned.1.call-start = ((), (), s32[]{:S(2)}) async-start(), calls=%async_computation.31 | async-start | bytes 10117120 | tf_op jit(solution)/shard_map/psum | solution.py:450
  (243 other events, 2993.5 us)
Sparse Core Ops, SparseCore 0:
  41.4 43.8 reduce-scatter.33
  89.1 41.1 reduce-scatter.31
  134.2 41.0 reduce-scatter.29
  185.1 24.5 all-gather.36
  212.0 24.7 all-gather.28
  238.8 28.0 all-gather.30
  269.4 23.9 all-gather.38
  295.7 93.9 all-gather.32
  391.9 54.3 all-gather.34
  466.6 54.0 all-reduce.38
  1608.2 58.6 all-reduce.34
  1757.8 42.9 reduce-scatter.21
  1811.8 42.8 reduce-scatter.19
  1858.5 43.5 reduce-scatter.23
  1913.6 27.5 all-gather.40
  1943.4 27.5 all-gather.42
  1972.7 27.5 all-gather.44
Sparse Core Ops, SparseCore 1:
  70.4 40.9 all-gather.26
  1945.6 214.8 all-reduce.32
  2162.7 47.4 reduce-scatter.25
  2212.5 68.9 reduce-scatter.35
  2283.9 193.7 reduce-scatter.27
  2480.7 780.2 all-reduce.30
  3265.2 116.7 all-reduce.36
where the time goes:
time: 3540 us; the launch traced here: 3510 us
  waiting for transfers between devices  1430 us (40%)
  local copies, waits for them, and re-layouts  980 us (28%)
  other arithmetic  435 us (12%)
  matrix products  389 us (11%)
  blocking collectives  246 us (7%)
    psum x1, waiting for transfers between devices, on_device(): table_total = lax.psum(table_grad, 'fsdp')  742 us
    gather x9, local copies, waits for them, and re-layouts, on_device(): jnp.take_along_axis(logits, jnp.where(teacher_inside, teacher_local, 0),...  689 us
    reduce_scatter x1, waiting for transfers between devices, on_device(): lax.psum_scatter(stacked[2], ('fsdp', 'tensor'), scatter_dimension=1, til...  196 us
    all_gather x9, blocking collectives, merged(): gathered = jax.tree.map(lambda a: lax.all_gather(a, axis), part)  154 us
    unnamed x15, other arithmetic  149 us
    all_gather x4, waiting for transfers between devices, on_device(): lax.all_gather(shortened(lowered), ('fsdp', 'tensor'), axis=1, tiled=True)  141 us
    dot_general x15, matrix products, across(): lax.dot_general(left, right, (((0,), (0,)), ((), ())), preferred_element_...  127 us
    unnamed x518, local copies, waits for them, and re-layouts  126 us
  transfers between devices with their start and end apart: 24, of which 15 were waited for; matrix products, arithmetic and copies ran while one was open for 22% of the time, Pallas kernels for 0%

commit v1 on v0

v1 whole, which is shorter than its diff:
```python
import functools

import jax
import jax.numpy as jnp
from jax import lax
from jax.experimental import pallas as pl
from jax.experimental.pallas import tpu as pltpu
from jax.sharding import PartitionSpec as P

QUERY_HEADS = 15
KEY_VALUE_HEADS = 5
GROUP = QUERY_HEADS // KEY_VALUE_HEADS
HEAD_SIZE = 64
FF = 2560
LAYER_COUNT = 1
TEACH = 64
STEP = 10


EPSILON = 1e-05
THETA = 100000.0
CLIP = 0.01
BETA_ONE = 0.9
BETA_TWO = 0.95
ADAM_EPSILON = 1e-08
DECAY = 0.1
RATE_MATRIX = 0.05
RATE_GAIN = 0.5
MASKED = -1e30
PLANE = ("context", "tensor")
SHARDS = ("fsdp", "tensor")
EVERYONE = ("fsdp", "context", "tensor")
LANES = 128
SUBLANES = 8


def matmul(left, right):
    return jnp.dot(left, right, preferred_element_type=jnp.float32)


def across(left, right):
    return lax.dot_general(
        left, right, (((0,), (0,)), ((), ())), preferred_element_type=jnp.float32
    )


def against(left, right):
    return lax.dot_general(
        left, right, (((1,), (1,)), ((), ())), preferred_element_type=jnp.float32
    )


def rounded(value_rows):
    return lax.optimization_barrier(value_rows.astype(jnp.bfloat16)).astype(jnp.float32)


def rmsnorm(value_rows, gain):
    return (
        value_rows
        * lax.rsqrt(jnp.mean(value_rows * value_rows, axis=-1, keepdims=True) + EPSILON)
        * gain
    )


def rotary_tables(places):
    half = HEAD_SIZE // 2
    freqs = THETA ** (-jnp.arange(half, dtype=jnp.float32) * 2.0 / HEAD_SIZE)
    angles = places.astype(jnp.float32)[:, None] * freqs[None, :]
    return jnp.cos(angles), jnp.sin(angles)


def rotate(heads, cosine, sine):
    half = HEAD_SIZE // 2
    first, second = heads[..., :half], heads[..., half:]
    return jnp.concatenate(
        [first * cosine - second * sine, first * sine + second * cosine], axis=-1
    )


def adamw(weight, grad, drift, power, rate, decay):
    moment = BETA_ONE * drift + (1.0 - BETA_ONE) * grad
    square = BETA_TWO * power + (1.0 - BETA_TWO) * grad * grad
    mean_hat = moment / (1.0 - BETA_ONE**STEP)
    square_hat = square / (1.0 - BETA_TWO**STEP)
    fresh = weight - rate * (mean_hat / (jnp.sqrt(square_hat) + ADAM_EPSILON) + decay * weight)
    return (fresh, moment, square)


def masked_scores(query, key, first_row, length):
    scores = against(query, key) * HEAD_SIZE ** (-0.5)
    count = query.shape[0] // GROUP
    row = lax.broadcasted_iota(jnp.int32, (count, key.shape[0]), 0) + first_row
    column = lax.broadcasted_iota(jnp.int32, (count, key.shape[0]), 1)
    allowed = (column <= row) & (column < length)
    allowed = jnp.concatenate([allowed] * GROUP, axis=0)
    return jnp.where(allowed, scores, MASKED)


def forward_kernel(bounds, q_ref, k_ref, v_ref, out_ref, total_ref):
    b = pl.program_id(0)
    scores = masked_scores(q_ref[...], k_ref[...], bounds[0], bounds[1 + b])
    top = jnp.max(scores, axis=-1, keepdims=True)
    powers = jnp.exp(scores - top)
    total = jnp.sum(powers, axis=-1, keepdims=True)
    chances = (powers * (1.0 / total)).astype(jnp.bfloat16)
    out_ref[...] = matmul(chances, v_ref[...]).astype(jnp.bfloat16)
    total_ref[...] = top + jnp.log(total)


def backward_kernel(bounds, q_ref, k_ref, v_ref, g_ref, total_ref, dq_ref, dk_ref, dv_ref):
    b = pl.program_id(0)
    query, key, value, grad = q_ref[...], k_ref[...], v_ref[...], g_ref[...]
    scores = masked_scores(query, key, bounds[0], bounds[1 + b])
    chances = jnp.exp(scores - total_ref[...])
    dv_ref[...] = across(chances.astype(jnp.bfloat16), grad)
    grad_chances = against(grad, value).astype(jnp.bfloat16).astype(jnp.float32)
    mean = jnp.sum(chances * grad_chances, axis=-1, keepdims=True)
    grad_scores = (chances * (grad_chances - mean)).astype(jnp.bfloat16)
    dq_ref[...] = matmul(grad_scores, key) * HEAD_SIZE ** (-0.5)
    dk_ref[...] = across(grad_scores, query) * HEAD_SIZE ** (-0.5)


def head_block(rows, width):
    return pl.BlockSpec((None, None, rows, width), lambda b, g, bounds: (b, g, 0, 0))


def attention_forward(bounds, query, key, value):
    batches, heads, rows, size = query.shape
    slots = key.shape[2]
    cost = pl.CostEstimate(
        flops=4 * batches * heads * rows * slots * size,
        bytes_accessed=2 * batches * heads * (2 * rows + 2 * slots) * size,
        transcendentals=batches * heads * rows * slots,
    )
    return pl.pallas_call(
        forward_kernel,
        name="attention_forward",
        grid_spec=pltpu.PrefetchScalarGridSpec(
            num_scalar_prefetch=1,
            grid=(batches, heads),
            in_specs=[head_block(rows, size), head_block(slots, size), head_block(slots, size)],
            out_specs=[head_block(rows, size), head_block(rows, 1)],
        ),
        out_shape=[
            jax.ShapeDtypeStruct(query.shape, jnp.bfloat16),
            jax.ShapeDtypeStruct((batches, heads, rows, 1), jnp.float32),
        ],
        cost_estimate=cost,
    )(bounds, query, key, value)


def attention_backward(bounds, query, key, value, grad, total):
    batches, heads, rows, size = query.shape
    slots = key.shape[2]
    cost = pl.CostEstimate(
        flops=10 * batches * heads * rows * slots * size,
        bytes_accessed=2 * batches * heads * (4 * rows + 6 * slots) * size,
        transcendentals=batches * heads * rows * slots,
    )
    return pl.pallas_call(
        backward_kernel,
        name="attention_backward",
        grid_spec=pltpu.PrefetchScalarGridSpec(
            num_scalar_prefetch=1,
            grid=(batches, heads),
            in_specs=[
                head_block(rows, size),
                head_block(slots, size),
                head_block(slots, size),
                head_block(rows, size),
                head_block(rows, 1),
            ],
            out_specs=[head_block(rows, size), head_block(slots, size), head_block(slots, size)],
        ),
        out_shape=[
            jax.ShapeDtypeStruct(query.shape, jnp.float32),
            jax.ShapeDtypeStruct(key.shape, jnp.float32),
            jax.ShapeDtypeStruct(key.shape, jnp.float32),
        ],
        cost_estimate=cost,
    )(bounds, query, key, value, grad, total)


def frequency_kernel(per_step, high_ref, low_ref, share_ref, out_ref):
    tiles = out_ref.shape[1] // LANES
    entries = high_ref.shape[-1]
    row = lax.broadcasted_iota(jnp.int32, (tiles * SUBLANES, entries), 0)
    lane = lax.broadcasted_iota(jnp.int32, (LANES, entries), 0)

    def one_group(group, carry):
        high = high_ref[pl.ds(group, 1), :]
        low = low_ref[pl.ds(group, 1), :]
        share = share_ref[...]
        left = jnp.where(row == high, share, 0.0).astype(jnp.bfloat16)
        right = jnp.where(lane == low, 1.0, 0.0).astype(jnp.bfloat16)
        counts = against(left, right)
        start = pl.multiple_of(group * SUBLANES, SUBLANES)
        for tile in range(tiles):
            out_ref[pl.ds(start, SUBLANES), tile * LANES : (tile + 1) * LANES] = counts[
                tile * SUBLANES : (tile + 1) * SUBLANES
            ]
        return carry

    lax.fori_loop(0, per_step, one_group, 0)


def frequencies_of(teacher, labels, start, vocab_rows):
    positions = teacher.shape[0]
    groups = positions // SUBLANES
    ids = jnp.concatenate([teacher, labels[:, None]], axis=1) - start
    inside = (ids >= 0) & (ids < vocab_rows)
    spot = (jnp.arange(positions, dtype=jnp.int32) % SUBLANES)[:, None]
    high = jnp.where(inside, (ids // LANES) * SUBLANES + spot, -1)
    low = jnp.where(inside, ids % LANES, -1)
    pad = -(SUBLANES * (TEACH + 1)) % LANES

    def packed(value):
        value = value.reshape(groups, SUBLANES * (TEACH + 1))
        return jnp.pad(value, ((0, 0), (0, pad)), constant_values=-1)

    share = jnp.where(
        jnp.arange(SUBLANES * (TEACH + 1)) % (TEACH + 1) == TEACH, 1.0, 1.0 / TEACH
    ).astype(jnp.float32)
    share = jnp.pad(share, (0, pad))[None, :]
    entries = share.shape[1]
    per_step = 8
    return pl.pallas_call(
        functools.partial(frequency_kernel, per_step),
        name="frequencies",
        grid=(groups // per_step,),
        in_specs=[
            pl.BlockSpec((per_step, entries), lambda i: (i, 0)),
            pl.BlockSpec((per_step, entries), lambda i: (i, 0)),
            pl.BlockSpec((1, entries), lambda i: (0, 0)),
        ],
        out_specs=pl.BlockSpec((per_step * SUBLANES, vocab_rows), lambda i: (i, 0)),
        out_shape=jax.ShapeDtypeStruct((positions, vocab_rows), jnp.float32),
        cost_estimate=pl.CostEstimate(
            flops=2 * groups * entries * vocab_rows * SUBLANES,
            bytes_accessed=4 * positions * vocab_rows,
            transcendentals=0,
        ),
    )(packed(high), packed(low), share)


def row_kernel(chunks, chunk, block, offsets, source, target, g_ref, dense_ref, out_ref, sum_ref, held):
    step = pl.program_id(0)

    @pl.when(step == 0)
    def _():
        sum_ref[...] = jnp.zeros_like(sum_ref)

        def clear(i, carry):
            held[pl.ds(i * 8, 8)] = jnp.zeros((8, SUBLANES, LANES), jnp.float32)
            return carry

        lax.fori_loop(0, held.shape[0] // 8, clear, 0)

    @pl.when(step < chunks)
    def _():
        def add(i, carry):
            row = target[i]
            held[row] = held[row] + g_ref[source[i] - step * chunk].astype(jnp.float32)
            return carry

        lax.fori_loop(offsets[step], offsets[step + 1], add, 0)

    @pl.when(step >= chunks)
    def _():
        start = pl.multiple_of((step - chunks) * block, block)
        width = out_ref.shape[1]
        for part in range(-(-width // LANES)):
            low, high = part * LANES, min(width, (part + 1) * LANES)
            total = held[pl.ds(start, block), part, :][:, : high - low] + dense_ref[:, low:high]
            out_ref[:, low:high] = total
            squares = total * total
            folded = jnp.sum(squares.reshape(block // SUBLANES, SUBLANES, high - low), axis=0)
            sum_ref[:, : high - low] += folded


def add_rows(rows, source, target, offsets, dense, chunk):
    vocab_rows, width = dense.shape
    chunks = rows.shape[0] // chunk
    block = 256
    blocks = vocab_rows // block
    return pl.pallas_call(
        functools.partial(row_kernel, chunks, chunk, block),
        name="add_rows",
        grid_spec=pltpu.PrefetchScalarGridSpec(
            num_scalar_prefetch=3,
            grid=(chunks + blocks,),
            in_specs=[
                pl.BlockSpec(
                    (chunk, SUBLANES, LANES), lambda i, *_: (jnp.minimum(i, chunks - 1), 0, 0)
                ),
                pl.BlockSpec((block, width), lambda i, *_: (jnp.maximum(i - chunks, 0), 0)),
            ],
            out_specs=[
                pl.BlockSpec((block, width), lambda i, *_: (jnp.maximum(i - chunks, 0), 0)),
                pl.BlockSpec((SUBLANES, LANES), lambda i, *_: (0, 0)),
            ],
            scratch_shapes=[pltpu.VMEM((vocab_rows, SUBLANES, LANES), jnp.float32)],
        ),
        out_shape=[
            jax.ShapeDtypeStruct((vocab_rows, width), jnp.float32),
            jax.ShapeDtypeStruct((SUBLANES, LANES), jnp.float32),
        ],
        compiler_params=pltpu.CompilerParams(vmem_limit_bytes=48 << 20),
        cost_estimate=pl.CostEstimate(
            flops=rows.shape[0] * 1024,
            bytes_accessed=2 * rows.size + 8 * dense.size,
            transcendentals=0,
        ),
    )(offsets, source, target, rows, dense)


def on_device(
    tokens,
    lengths,
    loss_positions,
    teacher_ids,
    label_ids,
    embedding,
    incoming,
    outgoing,
    expand,
    contract,
    scales,
    drift_embedding,
    incoming_first_moment,
    drift_outgoing,
    drift_expand,
    drift_contract,
    drift_scales,
    power_embedding,
    incoming_second_moment,
    power_outgoing,
    power_expand,
    power_contract,
    power_scales,
):
    ranks = lax.axis_size(PLANE)
    planes = lax.axis_size("fsdp")
    seq_rank = lax.axis_index(PLANE)
    plane = lax.axis_index("fsdp")
    batches, _, slots = tokens.shape
    rows = slots // ranks
    local = batches * rows
    first_row = seq_rank * rows
    vocab_rows, width = embedding.shape
    vocab_start = seq_rank * vocab_rows
    wanted = loss_positions.shape[2]
    own_count = batches * wanted
    count_all = planes * own_count
    query_width = QUERY_HEADS * HEAD_SIZE
    key_width = KEY_VALUE_HEADS * HEAD_SIZE
    number = 0

    table = embedding.astype(jnp.bfloat16)

    token_rows = tokens[:, 0]
    wire_ids = token_rows.reshape(batches, ranks, rows).transpose(1, 0, 2).reshape(-1) - vocab_start
    inside = (wire_ids >= 0) & (wire_ids < vocab_rows)
    found = jnp.take(table, jnp.where(inside, wire_ids, 0), axis=0)
    residual = lax.psum_scatter(
        jnp.where(inside[:, None], found, jnp.zeros((), jnp.bfloat16)),
        PLANE,
        scatter_dimension=0,
        tiled=True,
    ).astype(jnp.float32)

    def whole(master):
        return lax.all_gather(master.astype(jnp.bfloat16), SHARDS, axis=1, tiled=True)

    w_in = whole(incoming)[number]
    gains = whole(scales).astype(jnp.float32)
    w_out = whole(outgoing)[number]
    w_expand = whole(expand)[number]
    w_contract = whole(contract)[number]
    gain_attn, gain_ffn, gain_final = gains[0], gains[1], gains[2]

    teacher_all = lax.all_gather(teacher_ids[:, 0], "fsdp").reshape(count_all, TEACH)
    label_all = lax.all_gather(label_ids[:, 0], "fsdp").reshape(count_all)
    tokens_all = lax.all_gather(token_rows, "fsdp")
    frequencies = frequencies_of(teacher_all, label_all, vocab_start, vocab_rows)

    entry_ids = (
        tokens_all.reshape(planes, batches, ranks, rows).transpose(0, 2, 1, 3).reshape(-1)
        - vocab_start
    )
    entry_count = entry_ids.shape[0]
    entry_inside = (entry_ids >= 0) & (entry_ids < vocab_rows)
    entry_index = jnp.arange(entry_count, dtype=jnp.int32)
    source = lax.sort(jnp.where(entry_inside, entry_index, entry_count)) % entry_count
    target = jnp.clip(jnp.take(entry_ids, source), 0, vocab_rows - 1)
    chunk = 1024
    per_chunk = jnp.sum(entry_inside.reshape(-1, chunk).astype(jnp.int32), axis=1)
    offsets = jnp.concatenate([jnp.zeros((1,), jnp.int32), jnp.cumsum(per_chunk)])

    places = jnp.tile(first_row + jnp.arange(rows, dtype=jnp.int32), batches)
    cosine, sine = rotary_tables(places)
    cosine, sine = cosine[:, None, :], sine[:, None, :]
    bounds = jnp.concatenate([first_row[None].astype(jnp.int32), lengths[:, 0]])
    normed, attn_pull = jax.vjp(rmsnorm, residual, gain_attn)
    normed_low = normed.astype(jnp.bfloat16)
    joined = matmul(normed_low, w_in)
    queries = rotate(
        joined[:, :query_width].reshape(local, QUERY_HEADS, HEAD_SIZE), cosine, sine
    ).astype(jnp.bfloat16)
    keys = rotate(
        joined[:, query_width : query_width + key_width].reshape(
            local, KEY_VALUE_HEADS, HEAD_SIZE
        ),
        cosine,
        sine,
    ).astype(jnp.bfloat16)
    packed = jnp.concatenate(
        [
            keys.reshape(local, key_width),
            joined[:, query_width + key_width :].astype(jnp.bfloat16),
        ],
        axis=1,
    )
    gathered = (
        lax.all_gather(packed, PLANE)
        .reshape(ranks, batches, rows, 2, KEY_VALUE_HEADS, HEAD_SIZE)
        .transpose(3, 1, 4, 0, 2, 5)
        .reshape(2, batches, KEY_VALUE_HEADS, slots, HEAD_SIZE)
    )

    def to_heads(value):
        return (
            value.reshape(batches, rows, KEY_VALUE_HEADS, GROUP, HEAD_SIZE)
            .transpose(0, 2, 3, 1, 4)
            .reshape(batches, KEY_VALUE_HEADS, GROUP * rows, HEAD_SIZE)
        )

    def from_heads(value):
        return (
            value.reshape(batches, KEY_VALUE_HEADS, GROUP, rows, HEAD_SIZE)
            .transpose(0, 3, 1, 2, 4)
            .reshape(local, query_width)
        )

    query_heads = to_heads(queries)
    mixed, log_total_heads = attention_forward(bounds, query_heads, gathered[0], gathered[1])
    attended = from_heads(mixed)
    middle = residual + matmul(attended, w_out)
    normed_ffn, ffn_pull = jax.vjp(rmsnorm, middle, gain_ffn)
    normed_ffn_low = normed_ffn.astype(jnp.bfloat16)
    hidden, act_pull = jax.vjp(
        lambda both: jax.nn.silu(both[:, :FF]) * both[:, FF:], matmul(normed_ffn_low, w_expand)
    )
    hidden_low = hidden.astype(jnp.bfloat16)
    result = middle + matmul(hidden_low, w_contract)

    final, final_pull = jax.vjp(rmsnorm, result, gain_final)
    final_low = final.astype(jnp.bfloat16).reshape(batches, rows, width)
    spots = loss_positions[:, 0] % lengths[:, :1]
    picker = spots[:, :, None] == (first_row + jnp.arange(rows, dtype=jnp.int32))[None, None, :]
    picked = jnp.einsum(
        "bpr,brd->bpd", picker.astype(jnp.bfloat16), final_low, preferred_element_type=jnp.float32
    ).astype(jnp.bfloat16)
    chosen = lax.all_gather(
        lax.psum(picked.reshape(own_count, width), PLANE), "fsdp", axis=0, tiled=True
    )
    logits = against(chosen, table)
    top = jnp.max(logits, axis=1)
    total = jnp.sum(jnp.exp(logits - top[:, None]), axis=1)
    target_part = jnp.sum(frequencies * logits, axis=1)
    stats = lax.all_gather(jnp.stack([top, total, target_part]), PLANE)
    top_all = jnp.max(stats[:, 0], axis=0)
    total_all = jnp.sum(stats[:, 1] * jnp.exp(stats[:, 0] - top_all[None]), axis=0)
    target_all = jnp.sum(stats[:, 2], axis=0)
    log_total = top_all + jnp.log(total_all)
    teacher = teacher_ids[:, 0].reshape(own_count, TEACH)
    counts = jnp.sum((teacher[:, :, None] == teacher[:, None, :]).astype(jnp.float32), axis=-1)
    entropy_part = jnp.mean(jnp.log(counts / TEACH), axis=1)
    own = plane * own_count
    loss_sum = jnp.sum(
        entropy_part + lax.dynamic_slice_in_dim(2.0 * log_total - target_all, own, own_count)
    )
    grad_logits = (
        (2.0 * jnp.exp(logits - log_total[:, None]) - frequencies) / count_all
    ).astype(jnp.bfloat16)
    own_logits = lax.dynamic_slice_in_dim(grad_logits, own, own_count)
    grad_chosen = lax.psum(matmul(own_logits, table), PLANE).reshape(batches, wanted, width)
    grad_final = rounded(
        jnp.einsum(
            "bpr,bpd->brd",
            picker.astype(jnp.float32),
            grad_chosen,
            precision=lax.Precision.HIGHEST,
        ).reshape(local, width)
    )
    grad_residual, grad_gain_final = final_pull(grad_final)
    dense = across(grad_logits, chosen)

    branch = grad_residual.astype(jnp.bfloat16)
    grad_contract = across(hidden_low, branch)
    grad_hidden = rounded(against(branch, w_contract))
    grad_gate_up = act_pull(grad_hidden)[0].astype(jnp.bfloat16)
    grad_expand = across(normed_ffn_low, grad_gate_up)
    grad_normed = rounded(against(grad_gate_up, w_expand))
    grad_middle, grad_gain_ffn = ffn_pull(grad_normed)
    grad_middle = grad_middle + grad_residual
    branch = grad_middle.astype(jnp.bfloat16)
    grad_outgoing = across(attended, branch)
    grad_attended = against(branch, w_out).astype(jnp.bfloat16)
    dq, dk, dv = attention_backward(
        bounds, query_heads, gathered[0], gathered[1], to_heads(grad_attended), log_total_heads
    )
    grad_pair = (
        jnp.stack([dk, dv])
        .reshape(2, batches, KEY_VALUE_HEADS, ranks, rows, HEAD_SIZE)
        .transpose(3, 1, 4, 0, 2, 5)
        .reshape(ranks * local, 2 * key_width)
    )
    grad_pair = lax.psum_scatter(grad_pair, PLANE, scatter_dimension=0, tiled=True)
    grad_queries = rotate(
        from_heads(dq).reshape(local, QUERY_HEADS, HEAD_SIZE), cosine, -sine
    ).reshape(local, query_width)
    grad_keys = rotate(
        grad_pair[:, :key_width].reshape(local, KEY_VALUE_HEADS, HEAD_SIZE), cosine, -sine
    ).reshape(local, key_width)
    grad_joined = jnp.concatenate(
        [grad_queries, grad_keys, grad_pair[:, key_width:]], axis=1
    ).astype(jnp.bfloat16)
    grad_incoming = across(normed_low, grad_joined)
    grad_normed = rounded(against(grad_joined, w_in))
    grad_input, grad_gain_attn = attn_pull(grad_normed)
    grad_rows = (grad_input + grad_middle).astype(jnp.bfloat16)

    tile = SUBLANES * LANES
    padded = jnp.pad(grad_rows, ((0, 0), (0, tile - width))).reshape(local, SUBLANES, LANES)
    rows_all = lax.all_gather(padded, EVERYONE, axis=0, tiled=True)
    table_total, table_squares = add_rows(rows_all, source, target, offsets, dense, chunk)

    def reduced(grad):
        part = lax.psum_scatter(grad, SHARDS, scatter_dimension=1, tiled=True)
        return lax.psum(part, "context")

    layer_totals = (
        reduced(grad_incoming[None]),
        reduced(grad_outgoing[None]),
        reduced(grad_expand[None]),
        reduced(grad_contract[None]),
        reduced(jnp.stack([grad_gain_attn, grad_gain_ffn, grad_gain_final])),
    )
    lead_context = (lax.axis_index("context") == 0).astype(jnp.float32)
    lead_plane = (plane == 0).astype(jnp.float32)
    lead_seq = (seq_rank == 0).astype(jnp.float32)
    layer_square = sum((jnp.sum(grad * grad) for grad in layer_totals))
    sums = lax.psum(
        jnp.stack(
            [
                lead_context * layer_square + lead_plane * jnp.sum(table_squares),
                lead_seq * loss_sum,
            ]
        ),
        EVERYONE,
    )
    grad_norm = jnp.sqrt(sums[0])
    loss_value = sums[1] / count_all
    factor = CLIP / jnp.maximum(grad_norm, CLIP)
    weights = (embedding, incoming, outgoing, expand, contract, scales)
    grads = (table_total,) + layer_totals
    drifts = (
        drift_embedding,
        incoming_first_moment,
        drift_outgoing,
        drift_expand,
        drift_contract,
        drift_scales,
    )
    powers = (
        power_embedding,
        incoming_second_moment,
        power_outgoing,
        power_expand,
        power_contract,
        power_scales,
    )
    rates = (RATE_MATRIX, RATE_MATRIX, RATE_MATRIX, RATE_MATRIX, RATE_MATRIX, RATE_GAIN)
    decays = (DECAY, DECAY, DECAY, DECAY, DECAY, 0.0)
    updated = [
        adamw(
            weights[index],
            grads[index] * factor,
            drifts[index],
            powers[index],
            rates[index],
            decays[index],
        )
        for index in range(6)
    ]
    return (
        (loss_value, grad_norm)
        + tuple(entry[0] for entry in updated)
        + tuple(entry[1] for entry in updated)
        + tuple(entry[2] for entry in updated)
    )


def solution(mesh):
    ids = P(None, "fsdp", None)
    vocab = P(PLANE, None)
    matrix = P(None, SHARDS, None)
    state = (vocab, matrix, matrix, matrix, matrix, P(None, SHARDS))
    in_specs = (ids, P(None, "fsdp"), ids, P(None, "fsdp", None, None), ids) + state * 3
    out_specs = (P(), P()) + state * 3
    return jax.shard_map(
        on_device, mesh=mesh, in_specs=in_specs, out_specs=out_specs, check_vma=False
    )
```

time: 3540 us -> 1900 us (0.54)
  local copies, waits for them, and re-layouts: 980 us -> 371 us
  waiting for transfers between devices: 1430 us -> 828 us
  matrix products: 389 us -> 138 us
  other arithmetic: 435 us -> 209 us
  Pallas kernels: 0 us -> 170 us
  blocking collectives: 246 us -> 143 us
    psum x4 -> x3, waiting for transfers between devices: 908 us -> 113 us  [the longest x1 58.1 us: on_device(): lax.psum(matmul(own_logits, table), PLANE).reshape(batches, wanted, width)]
    gather x15 -> x2, local copies, waits for them, and re-layouts: 729 us -> 90.3 us  [the longest x1 68.2 us: on_device(): target = jnp.clip(jnp.take(entry_ids, source), 0, vocab_rows - 1)]
    unnamed x29 -> x19, waiting for transfers between devices: 98.3 us -> 288 us
    pallas_call x0 -> x4, Pallas kernels: none -> 170 us  [the longest x1 61.2 us: frequencies_of(): pl.pallas_call(functools.partial(frequency_kernel, per_step), name='frequ...]
    unnamed x15 -> x3, other arithmetic: 149 us -> 0.03 us
    dot_general x108 -> x2, matrix products: 142 us -> 3.61 us  [the longest x1 2.21 us: on_device(): jnp.einsum('bpr,bpd->brd', picker.astype(jnp.float32), grad_chosen, preci...]
    scatter-add x6 -> x0, other arithmetic: 121 us -> none  [the longest x3 62 us: on_device(): jax.ops.segment_sum(grad_tokens.astype(jnp.float32), slots, num_segments=...]
    all_gather x10 -> x5, blocking collectives: 168 us -> 64.1 us  [the longest x1 16.7 us: on_device(): lax.all_gather(teacher_ids[:, 0], 'fsdp').reshape(count_all, TEACH)]
  transfers between devices with their start and end apart: 24 -> 16, of which waited for: 15 -> 11; matrix products, arithmetic and copies ran while one was open for 22% -> 15% of each run, Pallas kernels for 0% -> 4%
where the time goes in v1:
time: 1900 us; the launch traced here: 1890 us
  waiting for transfers between devices  828 us (44%)
  local copies, waits for them, and re-layouts  371 us (20%)
  other arithmetic  209 us (11%)
  Pallas kernels  170 us (9%)
  blocking collectives  143 us (8%)
  matrix products  138 us (7%)
  between operations  26.9 us (1%)
    unnamed x19, waiting for transfers between devices  288 us
    reduce_scatter x2, waiting for transfers between devices, reduced(): part = lax.psum_scatter(grad, SHARDS, scatter_dimension=1, tiled=True)  196 us
    unnamed x143, local copies, waits for them, and re-layouts  159 us
    all_gather x4, waiting for transfers between devices, whole(): lax.all_gather(master.astype(jnp.bfloat16), SHARDS, axis=1, tiled=True)  107 us
    sub x6, other arithmetic, adamw(): weight - rate * (mean_hat / (jnp.sqrt(square_hat) + ADAM_EPSILON) + decay...  75.7 us
    all_gather x1, waiting for transfers between devices, on_device(): rows_all = lax.all_gather(padded, EVERYONE, axis=0, tiled=True)  72.1 us
    gather x1, local copies, waits for them, and re-layouts, on_device(): target = jnp.clip(jnp.take(entry_ids, source), 0, vocab_rows - 1)  68.2 us
    pallas_call x1, Pallas kernels, frequencies_of(): pl.pallas_call(functools.partial(frequency_kernel, per_step), name='frequ...  61.2 us
  transfers between devices with their start and end apart: 16, of which 11 were waited for; matrix products, arithmetic and copies ran while one was open for 15% of the time, Pallas kernels for 4%

profile of v1, /device:TPU:0, one launch (start us, length us, event | category | flops | bytes accessed | tf_op | source)
XLA Modules:
  0.0 1886.9 jit_solution(9139693008822373448)
XLA Ops:
  8.9 24.1 %copy.206 = f32[6144,960]{1,0:T(8,128)} copy(f32[6144,960]{0,1:T(8,128)} %param.28) | data formatting | bytes 47185920 | tf_op args[5]
  46.4 22.1 %gather_fusion = bf16[3072,960]{1,0:T(8,128)(2,1)} fusion(bf16[6144,960]{1,0:T(8,128)(2,1)} %convert_element_type.120, s32[3072]{0:T(1024)S(1)} %broadcast_clamp_fusion), kind=kCustom, calls=%fused_computation | custom fusion | bytes 11808768 | tf_op jit(solution)/shard_map/jit(_take)/gather | solution.py:364
  91.8 48.1 %reduce-scatter.18.cloned.1.call-done = bf16[384,960]{1,0:T(8,128)(2,1)} async-done(((bf16[3072,960]{1,0:T(8,128)(2,1)}), bf16[384,960]{1,0:T(8,128)(2,1)}) %reduce-scatter.18.cloned.1.call-update) | async-done | bytes 737296
  157.4 27.1 %all-gather.27.cloned.1.call-done = bf16[3072,640]{0,1:T(8,128)(2,1)} async-done(((bf16[384,640]{0,1:T(8,128)(2,1)}), bf16[3072,640]{0,1:T(8,128)(2,1)}) %all-gather.27.cloned.1.call-update) | async-done | bytes 3932176 | tf_op jit(solution)/shard_map/all_gather | solution.py:425
  217.6 23.6 %attention_forward.1 = (bf16[3,5,384,64]{3,2,1,0:T(8,128)(2,1)}, f32[3,5,384,1]{3,2,1,0:T(8,128)}) custom-call(s32[4]{0:T(128)} %pad_add_fusion.bounds, bf16[3,5,384,64]{3,2,1,0:T(8,128)(2,1)} %bitcast.208, bf16[3,5,1024,64]{3,2,1,0:T(8,128)(2,1)} %bitcast.189, bf16[3,5,1024,64]{3,2,1,0:T(8,128)(2,1)} %bitcast.191), custom_call_target="tpu_custom_call" | custom-call | flops 1509949440 | bytes 5406720 | tf_op jit(solution)/shard_map/attention_forward/pallas_call | solution.py:135
  247.1 63.2 %all-gather.19.cloned.1.call-done = bf16[1,960,5120]{2,1,0:T(8,128)(2,1)} async-done(((bf16[1,120,5120]{2,1,0:T(8,128)(2,1)}), bf16[1,960,5120]{2,1,0:T(8,128)(2,1)}) %all-gather.19.cloned.1.call-update) | async-done | bytes 9830416 | tf_op jit(solution)/shard_map/all_gather | solution.py:373
  323.4 43.4 %all-gather.21.cloned.1.call-done = bf16[1,2560,960]{2,1,0:T(8,128)(2,1)} async-done(((bf16[1,320,960]{2,1,0:T(8,128)(2,1)}), bf16[1,2560,960]{2,1,0:T(8,128)(2,1)}) %all-gather.21.cloned.1.call-update) | async-done | bytes 4915216 | tf_op jit(solution)/shard_map/all_gather | solution.py:373
  378.9 54.5 %all-reduce.15.cloned.1.call-done = bf16[384,960]{1,0:T(8,128)(2,1)} async-done(((bf16[384,960]{1,0:T(8,128)(2,1)}), bf16[384,960]{1,0:T(8,128)(2,1)}) %all-reduce.15.cloned.1.call-update) | async-done | bytes 737296 | tf_op jit(solution)/shard_map/psum | solution.py:465
  433.5 16.7 all-gather.1
  466.8 61.2 %frequencies.1 = f32[1536,6144]{1,0:T(8,128)} custom-call(s32[192,640]{1,0:T(8,128)} %pad.21.high_ref, s32[192,640]{1,0:T(8,128)} %pad.22.low_ref, f32[1,640]{1,0:T(1,128)} %broadcast_in_dim.95.share_ref), custom_call_target="tpu_custom_call" | custom-call | flops 12079595520 | bytes 37748736 | tf_op jit(solution)/shard_map/frequencies/pallas_call | solution.py:227
  528.0 28.3 %fusion.119 = (f32[1536]{0:T(1024)S(1)}, f32[1536,6144]{1,0:T(8,128)}) fusion(bf16[1536,960]{1,0:T(8,128)(2,1)} %all-gather.23.cloned.1.call-done, bf16[6144,960]{1,0:T(8,128)(2,1)} %convert_element_type.120), kind=kOutput, calls=%fused_computation.236 | convolution fusion | flops 18128828416 | bytes 52500480 | tf_op jit(solution)/shard_map/dot_general | solution.py:48
  556.3 24.0 %exponential_reduce_fusion = (f32[1536]{0:T(1024)S(1)}, f32[1536]{0:T(1024)S(1)}) fusion(f32[1536,6144]{1,0:T(8,128)} %get-tuple-element.206, f32[1536]{0:T(1024)S(1)} %get-tuple-element.205, f32[1536,6144]{1,0:T(8,128)} %frequencies.1), kind=kLoop, calls=%fused_computation.5 | loop fusion | flops 37745664 | bytes 75515904 | tf_op jit(solution)/shard_map/reduce_sum | solution.py:469
  589.5 31.7 %multiply_convert_fusion = bf16[1536,6144]{1,0:T(8,128)(2,1)} fusion(f32[1536,6144]{1,0:T(8,128)} %frequencies.1, f32[1536,6144]{1,0:T(8,128)} %get-tuple-element.206, f32[1536]{0:T(1024)S(1)} %log_add_fusion), kind=kLoop, calls=%fused_computation.3 | loop fusion | flops 47185920 | bytes 94377984 | tf_op jit(solution)/shard_map/convert_element_type | solution.py:485
  635.7 58.1 %all-reduce.17.cloned.1.call-done = f32[3,128,960]{1,2,0:T(8,128)} async-done(((f32[3,128,960]{1,2,0:T(8,128)}), f32[3,128,960]{1,2,0:T(8,128)}) %all-reduce.17.cloned.1.call-update) | async-done | bytes 1474576 | tf_op jit(solution)/shard_map/psum | solution.py:487
  726.9 28.9 %attention_backward.1 = (f32[3,5,384,64]{3,2,1,0:T(8,128)}, f32[3,5,1024,64]{3,2,1,0:T(8,128)}, f32[3,5,1024,64]{3,2,1,0:T(8,128)}) custom-call(s32[4]{0:T(128)} %pad_add_fusion.bounds, bf16[3,5,384,64]{3,2,1,0:T(8,128)(2,1)} %bitcast.209, bf16[3,5,1024,64]{3,2,1,0:T(8,128)(2,1)} %bitcast.190, bf16[3,5,1024,64]{3,2,1,0:T(8,128)(2,1)} %bitcast.192, ...), custom_call_target="tpu_custom_call" | custom-call | flops 3774873600 | bytes 14745600 | tf_op jit(solution)/shard_map/attention_backward/pallas_call | solution.py:160
  807.5 22.2 %copy.228 = f32[1,2560,960]{2,0,1:T(1,128)} copy(f32[1,2560,960]{1,2,0:T(8,128)} %convolution_bitcast_fusion.1) | data formatting | bytes 19660800 | tf_op jit(solution)/shard_map/broadcast_in_dim | solution.py:547
  842.6 24.5 %reduce-scatter.12.cloned.1.call-done = f32[384,640]{0,1:T(8,128)} async-done(((f32[3072,640]{0,1:T(8,128)}), f32[384,640]{0,1:T(8,128)}) %reduce-scatter.12.cloned.1.call-update) | async-done | bytes 983056 | tf_op jit(solution)/shard_map/reduce_scatter | solution.py:519
  874.1 13.7 convolution_bitcast_fusion
  889.6 231.4 %all-reduce.19.cloned.1.call-done = f32[1,2560,960]{2,0,1:T(1,128)} async-done(((f32[1,2560,960]{2,0,1:T(1,128)}), f32[1,2560,960]{2,0,1:T(1,128)}) %all-reduce.19.cloned.1.call-update) | async-done | bytes 9830416
  1133.3 196.4 %reduce-scatter.16.cloned.1.call-done = f32[1,120,5120]{2,1,0:T(8,128)} async-done(((f32[1,960,5120]{2,1,0:T(8,128)}), f32[1,120,5120]{2,1,0:T(8,128)}) %reduce-scatter.16.cloned.1.call-update) | async-done | bytes 2457616 | tf_op jit(solution)/shard_map/reduce_scatter | solution.py:540
  1360.4 68.2 %gather_fusion.1 = s32[12288]{0:T(1024)S(1)} fusion(s32[12288]{0:T(1024)S(1)} %sub.158, s32[12288]{0:T(1024)S(1)} %fusion.86), kind=kCustom, calls=%fused_computation.1 | custom fusion | bytes 147456 | tf_op jit(solution)/shard_map/jit(_take)/gather | solution.py:395
  1428.7 24.5 %copy.235 = f32[6144,960]{1,0:T(8,128)} copy(f32[6144,960]{0,1:T(8,128)} %param.34) | data formatting | bytes 47185920 | tf_op args[11]
  1456.6 25.8 %fusion.120.dense_ref = f32[6144,960]{1,0:T(8,128)} fusion(bf16[1536,6144]{1,0:T(8,128)(2,1)} %multiply_convert_fusion, bf16[1536,960]{1,0:T(8,128)(2,1)S(1)} %copy-done.58), kind=kOutput, calls=%fused_computation.237 | convolution fusion | flops 18119393280 | bytes 45416448 | tf_op jit(solution)/shard_map/dot_general | solution.py:42
  1482.4 27.5 %all-reduce.8 = f32[3,960]{1,0:T(4,128)S(1)} all-reduce(f32[3,960]{1,0:T(4,128)S(1)} %pad_maximum_fusion.7), channel_id=13, replica_groups=mesh['fsdp'=4,'context'=4,'tensor'=2] {'fsdp','tensor'}, use_global_device_ids=true, to_apply=%region_29.30.clone | all-reduce | flops 2880 | bytes 23040
  1532.0 72.1 %all-gather.25.cloned.1.call-done.g_ref = bf16[12288,8,128]{2,1,0:T(8,128)(2,1)} async-done(((bf16[384,8,128]{2,1,0:T(8,128)(2,1)}), bf16[12288,8,128]{2,1,0:T(8,128)(2,1)}) %all-gather.25.cloned.1.call-update) | async-done | bytes 25165840 | tf_op jit(solution)/shard_map/all_gather | solution.py:536
  1604.1 55.9 %add_rows.1 = (f32[6144,960]{1,0:T(8,128)}, f32[8,128]{1,0:T(8,128)S(1)}) custom-call(s32[13]{0:T(128)S(1)} %pad_add_fusion.1.offsets, s32[12288]{0:T(1024)S(1)} %get-tuple-element.190.source, s32[12288]{0:T(1024)S(1)} %get-tuple-element.189.target, bf16[12288,8,128]{2,1,0:T(8,128)(2,1)} %all-gather.25.cloned.1.call-done.g_ref, f32[6144,960]{1,0:T(8,128)} %fusion.120.dense_ref), custom_call_target="tpu_custom_call" | custom-call | flops 12582912 | bytes 72351744 | tf_op jit(solution)/shard_map/add_rows/pallas_call | solution.py:286
  1661.3 24.1 %copy.236 = f32[6144,960]{1,0:T(8,128)} copy(f32[6144,960]{0,1:T(8,128)} %param.40) | data formatting | bytes 47185920 | tf_op args[17]
  1685.4 41.5 %psum.63 = f32[2]{0:T(128)S(1)} all-reduce(f32[2]{0:T(128)S(1)} %pad_maximum_fusion.8), channel_id=1, replica_groups=mesh['fsdp'=4,'context'=4,'tensor'=2] {'fsdp','context','tensor'}, use_global_device_ids=true, to_apply=%region_42.43 | all-reduce | flops 2 | bytes 16 | tf_op jit(solution)/shard_map/psum | solution.py:554
  1728.2 60.1 %multiply_subtract_fusion = (f32[6144,960]{1,0:T(8,128)}, f32[6144,960]{1,0:T(8,128)}, f32[6144,960]{1,0:T(8,128)}) fusion(f32[6144,960]{1,0:T(8,128)} %copy.206, f32[6144,960]{1,0:T(8,128)} %get-tuple-element.36, f32[]{:T(128)S(6)} %div.198, f32[6144,960]{1,0:T(8,128)} %copy.235, f32[6144,960]{1,0:T(8,128)} %copy.236), kind=kLoop, calls=%fused_computation.7 | loop fusion | flops 94371840 | bytes 165150720 | tf_op jit(solution)/shard_map/sub | solution.py:85
  1788.3 24.0 %copy.239 = f32[6144,960]{0,1:T(8,128)} copy(f32[6144,960]{1,0:T(8,128)} %get-tuple-element.166) | data formatting | bytes 47185920
  1812.3 24.0 %copy.240 = f32[6144,960]{0,1:T(8,128)} copy(f32[6144,960]{1,0:T(8,128)} %get-tuple-element.167) | data formatting | bytes 47185920
  1836.3 24.1 %copy.241 = f32[6144,960]{0,1:T(8,128)} copy(f32[6144,960]{1,0:T(8,128)} %get-tuple-element.168) | data formatting | bytes 47185920
  (326 shorter events, 344.9 us)
Async XLA Ops:
  8.0 131.9 %reduce-scatter.18.cloned.1.call-start = ((), (), s32[]{:S(2)}) async-start(), calls=%async_computation.17 | async-start | bytes 7077888
  75.3 66.4 %all-gather.15.cloned.1.call-start = ((), (), s32[]{:S(2)}) async-start(), calls=%async_computation.5 | async-start | bytes 3594240 | tf_op jit(solution)/shard_map/all_gather | solution.py:373
  77.2 107.3 %all-gather.27.cloned.1.call-start = ((), (), s32[]{:S(2)}) async-start(), calls=%async_computation.16 | async-start | bytes 4423680 | tf_op jit(solution)/shard_map/all_gather | solution.py:425
  90.9 54.8 %copy-start.40 = (f32[1,960]{1,0:T(1,128)}, f32[1,960]{1,0:T(1,128)S(1)}, u32[]{:S(2)}) copy-start(f32[1,960]{1,0:T(1,128)S(1)} %get-tuple-element.193) | copy-start | bytes 11524
  90.9 219.4 %copy-start.31 = (f32[1,960]{1,0:T(1,128)}, f32[1,960]{1,0:T(1,128)S(1)}, u32[]{:S(2)}) copy-start(f32[1,960]{1,0:T(1,128)S(1)} %get-tuple-element.192) | copy-start | bytes 11524
  91.8 55.4 %copy-start.28 = (f32[384,32]{0,1:T(8,128)}, f32[384,32]{0,1:T(8,128)S(1)}, u32[]{:S(2)}) copy-start(f32[384,32]{0,1:T(8,128)S(1)} %get-tuple-element.198) | copy-start | bytes 147460
  91.8 55.4 %copy-start.34 = (f32[384,32]{0,1:T(8,128)}, f32[384,32]{0,1:T(8,128)S(1)}, u32[]{:S(2)}) copy-start(f32[384,32]{0,1:T(8,128)S(1)} %get-tuple-element.197) | copy-start | bytes 147460
  141.4 102.5 %copy-start.3 = (bf16[384,960]{0,1:T(8,128)(2,1)}, bf16[384,960]{0,1:T(8,128)(2,1)S(1)}, u32[]{:S(2)}) copy-start(bf16[384,960]{0,1:T(8,128)(2,1)S(1)} %copy.246) | copy-start | bytes 2211844
  148.2 95.7 %all-gather.17.cloned.1.call-start = ((), (), s32[]{:S(2)}) async-start(), calls=%async_computation.6 | async-start | bytes 2211840 | tf_op jit(solution)/shard_map/all_gather | solution.py:373
  149.0 161.3 %all-gather.19.cloned.1.call-start = ((), (), s32[]{:S(2)}) async-start(), calls=%async_computation.7 | async-start | bytes 11059200 | tf_op jit(solution)/shard_map/all_gather | solution.py:373
  152.1 214.7 %all-gather.21.cloned.1.call-start = ((), (), s32[]{:S(2)}) async-start(), calls=%async_computation.8 | async-start | bytes 5898240 | tf_op jit(solution)/shard_map/all_gather | solution.py:373
  153.1 280.3 %all-reduce.15.cloned.1.call-start = ((), (), s32[]{:S(2)}) async-start(), calls=%async_computation.9 | async-start | bytes 1572864 | tf_op jit(solution)/shard_map/psum | solution.py:465
  247.0 70.6 %copy-start.50 = (f32[384]{0:T(512)}, f32[384]{0:T(512)S(1)}, u32[]{:S(2)}) copy-start(f32[384]{0:T(512)S(1)} %get-tuple-element.201) | copy-start | bytes 4612
  247.1 119.7 %copy-start.1 = (f32[384,960]{0,1:T(8,128)}, f32[384,960]{0,1:T(8,128)S(1)}, u32[]{:S(2)}) copy-start(f32[384,960]{0,1:T(8,128)S(1)} %get-tuple-element.202) | copy-start | bytes 4423684
  247.1 70.6 %copy-start.38 = (f32[384]{0:T(512)}, f32[384]{0:T(512)S(1)}, u32[]{:S(2)}) copy-start(f32[384]{0:T(512)S(1)} %fusion.100) | copy-start | bytes 4612
  375.1 58.4 %copy-start.36 = (s32[3,1,128,64]{2,3,1,0:T(8,128)S(1)}, s32[3,1,128,64]{2,3,1,0:T(8,128)}, u32[]{:S(2)}) copy-start(s32[3,1,128,64]{2,3,1,0:T(8,128)} %param.26) | copy-start | bytes 294916
  376.5 74.1 %copy-start.57 = (s32[3,1,128]{2,1,0:T(1,128)S(1)}, s32[3,1,128]{2,1,0:T(1,128)}, u32[]{:S(2)}) copy-start(s32[3,1,128]{2,1,0:T(1,128)} %param.27) | copy-start | bytes 4612
  378.8 149.2 %all-gather.23.cloned.1.call-start = ((), (), s32[]{:S(2)}) async-start(), calls=%async_computation.10 | async-start | bytes 3932160 | tf_op jit(solution)/shard_map/all_gather | solution.py:464
  433.5 260.3 %all-reduce.17.cloned.1.call-start = ((), (), s32[]{:S(2)}) async-start(), calls=%async_computation.11 | async-start | bytes 2949120 | tf_op jit(solution)/shard_map/psum | solution.py:487
  589.5 31.7 %copy-start.45 = (f32[1536]{0:T(1024)}, f32[1536]{0:T(1024)S(1)}, u32[]{:S(2)}) copy-start(f32[1536]{0:T(1024)S(1)} %log_add_fusion) | copy-start | bytes 18436
  635.6 231.5 %reduce-scatter.12.cloned.1.call-start = ((), (), s32[]{:S(2)}) async-start(), calls=%async_computation.12 | async-start | bytes 8847360 | tf_op jit(solution)/shard_map/reduce_scatter | solution.py:519
  798.3 322.8 %all-reduce.19.cloned.1.call-start = ((), (), s32[]{:S(2)}) async-start(), calls=%async_computation.18 | async-start | bytes 20971520
  829.7 294.9 %reduce-scatter.14.cloned.1.call-start = ((), (), s32[]{:S(2)}) async-start(), calls=%async_computation.13 | async-start | bytes 4423680 | tf_op jit(solution)/shard_map/reduce_scatter | solution.py:540
  835.8 297.5 %reduce-scatter.20.cloned.1.call-start = ((), (), s32[]{:S(2)}) async-start(), calls=%async_computation.19 | async-start | bytes 7188480
  842.4 26.9 %copy-start.4 = (bf16[384,960]{0,1:T(8,128)(2,1)S(1)}, bf16[384,960]{0,1:T(8,128)(2,1)}, u32[]{:S(2)}) copy-start(bf16[384,960]{0,1:T(8,128)(2,1)} %copy-done.3) | copy-start | bytes 2211844
  842.4 26.9 %copy-start.41 = (f32[1,960]{1,0:T(1,128)S(1)}, f32[1,960]{1,0:T(1,128)}, u32[]{:S(2)}) copy-start(f32[1,960]{1,0:T(1,128)} %copy-done.40) | copy-start | bytes 11524
  842.5 26.9 %copy-start.43 = (f32[384]{0:T(512)S(1)}, f32[384]{0:T(512)}, u32[]{:S(2)}) copy-start(f32[384]{0:T(512)} %copy-done.42) | copy-start | bytes 4612
  874.0 455.7 %reduce-scatter.16.cloned.1.call-start = ((), (), s32[]{:S(2)}) async-start(), calls=%async_computation.14 | async-start | bytes 22118400 | tf_op jit(solution)/shard_map/reduce_scatter | solution.py:540
  887.8 633.2 %all-reduce.21.cloned.1.call-start = ((), (), s32[]{:S(2)}) async-start(), calls=%async_computation.20 | async-start | bytes 10117120 | tf_op jit(solution)/shard_map/psum | solution.py:541
  1329.8 274.3 %all-gather.25.cloned.1.call-start = ((), (), s32[]{:S(2)}) async-start(), calls=%async_computation.15 | async-start | bytes 25952256 | tf_op jit(solution)/shard_map/all_gather | solution.py:536
  1428.7 27.9 %copy-start.58 = (bf16[1536,960]{1,0:T(8,128)(2,1)S(1)}, bf16[1536,960]{1,0:T(8,128)(2,1)}, u32[]{:S(2)}) copy-start(bf16[1536,960]{1,0:T(8,128)(2,1)} %all-gather.23.cloned.1.call-done) | copy-start | bytes 8847364
  1836.3 28.2 %copy-start.25 = (f32[1,120,960]{2,1,0:T(8,128)S(1)}, f32[1,120,960]{2,1,0:T(8,128)}, u32[]{:S(2)}) copy-start(f32[1,120,960]{2,1,0:T(8,128)} %get-tuple-element.148) | copy-start | bytes 1382404
  (50 other events, 271.4 us)
Sparse Core Ops, SparseCore 0:
  75.4 64.4 reduce-scatter.17
  148.3 36.1 all-gather.26
  186.7 28.0 all-gather.16
  216.9 93.3 all-gather.18
  312.4 54.3 all-gather.20
  379.0 54.4 all-reduce.14
  635.7 58.0 all-reduce.16
  798.4 68.6 reduce-scatter.11
  869.4 109.6 reduce-scatter.13
  981.3 151.9 reduce-scatter.19
  1136.2 193.4 reduce-scatter.15
Sparse Core Ops, SparseCore 1:
  78.0 41.1 all-gather.14
  433.5 64.3 all-gather.22
  829.8 291.2 all-reduce.18
  1329.8 116.4 all-reduce.20
  1449.7 154.3 all-gather.24
